TPU v7x, 32 devices: a whole 2x2x4 slice. The times are simulated.
32 devices in a mesh: nodes: 32 (over z, y, x, core).
Axes of the slice: x: 2, y: 2, z: 4, core: 2. Of those that a mesh axis runs over, the one named last changes fastest.
Arguments:
- rhs: bfloat16 [4, 20480, 256], P(None, 'nodes'), may hold values from -6 to 6
- inv_diag: bfloat16 [4, 20480, 640], P(None, 'nodes'), as said below
- factor: bfloat16 [3, 49152, 640], P(None, 'nodes'), may hold values from -0.15625 to 0.15625
- tile_list: int32 [3, 32, 12], P(None, 'nodes'), may hold values from 0 to 239, as said below
- live_count: int32 [3, 32], P(None, 'nodes'), may hold values from 4 to 12, as said below
Outputs:
- solution: float32 [4, 20480, 256], P(None, 'nodes')
Inputs may be any that keep to these rules, and one draw needn't show every extreme that they name: `tile_list`: entries at first index i name tiles of levels 0 to i only: they are below (i + 1) * 2 * 8 * 5. `live_count`: in every level some supernode has all 12 slots in use. `inv_diag`: each 640 by 640 block is upper triangular: zero below its diagonal, diagonal entries between 0.5 and 2.
All inputs are finite; a program needn't handle non-finite values.
Results may differ from a plain program's by a relative error of at most 0.004.
Values may be sent and summed in bfloat16 or wider, within the bound.
No kernel may reach another device: no remote copies, remote signals or barrier semaphores. Data moves between devices by JAX's collectives and lax.ppermute only.
A program may use at most 128 MiB of HBM per device.

v0:
```python
import functools

import jax
import jax.numpy as jnp
from jax import lax
from jax.experimental import pallas as pl
from jax.experimental.pallas import tpu as pltpu
from jax.sharding import PartitionSpec as P

GROUP = 8
CORES = 2
CHIPS = GROUP // CORES


HBM = pl.BlockSpec(memory_space=pltpu.HBM)
VMEM = pl.BlockSpec(memory_space=pltpu.VMEM)
SMEM = pl.BlockSpec(memory_space=pltpu.SMEM)
PARAMS = pltpu.CompilerParams(vmem_limit_bytes=16 * 2**20)


LATE = (2, 3)
ORDER = tuple(hop for hop in range(CHIPS) if hop not in LATE) + LATE


def send(value, hop, step=0):
    size = lax.axis_size("nodes")
    route = [(i, ((i ^ (hop * CORES)) + step * GROUP) % size) for i in range(size)]
    return lax.ppermute(value, "nodes", route)


def swap(value):
    size = lax.axis_size("nodes")
    return lax.ppermute(value, "nodes", [(i, i ^ 1) for i in range(size)])


def call(kernel, out_shape, in_specs, out_specs, flops, moved, scratch=(), aliases=None):
    return pl.pallas_call(
        kernel,
        out_shape=out_shape,
        in_specs=in_specs,
        out_specs=out_specs,
        scratch_shapes=list(scratch),
        input_output_aliases=aliases or {},
        compiler_params=PARAMS,
        cost_estimate=pl.CostEstimate(flops=flops, bytes_accessed=moved, transcendentals=0),
    )


def chip_place():
    return lax.axis_index("nodes") % GROUP // CORES


def run_copies(copies):
    for copy in copies:
        copy.start()
    for copy in copies:
        copy.wait()


def solve_rows(inv_ref, reduced_ref, x_ref, piece_refs, tile, row_done=None):
    width = inv_ref.shape[0]
    quarter = tile // CHIPS
    per_node = width // tile
    for i in reversed(range(per_node)):
        x_ref[i * tile : (i + 1) * tile, :] = jnp.dot(
            inv_ref[i * tile : (i + 1) * tile, i * tile :],
            reduced_ref[i * tile :, :],
            preferred_element_type=jnp.float32,
        )
        if row_done is not None:
            row_done(i)
    for relative, piece_ref in enumerate(piece_refs):
        first = (chip_place() ^ relative) * quarter
        for i in range(per_node):
            start = pl.multiple_of(i * tile + first, quarter)
            piece_ref[i] = x_ref[pl.ds(start, quarter), :].astype(jnp.bfloat16)


def places_of(entries, relative, levels, pool, per_node):
    def whole_parts(value, size, most):
        return sum((value >= size * k).astype(jnp.int32) for k in range(1, most))

    position = lax.axis_index("nodes") % GROUP
    chip, core = position // CORES, position % CORES
    named = whole_parts(entries, pool, levels)
    inside = entries - named * pool
    group = whole_parts(inside, GROUP * per_node, 2)
    inside = inside - group * (GROUP * per_node)
    member = whole_parts(inside, per_node, GROUP)
    row = inside - member * per_node
    member_chip = whole_parts(member, CORES, CHIPS)
    side = CORES * group + ((member - member_chip * CORES) ^ core)
    return named * pool + (side * CHIPS + (member_chip ^ (chip ^ relative))) * per_node + row


def first_kernel(tile, list_hbm, rhs_hbm, inv_hbm, x_ref, *refs):
    piece_refs, noted_refs = refs[:CHIPS], refs[CHIPS:-5]
    rhs_ref, inv_ref, list_ref, note_ref, sems = refs[-5:]
    run_copies(
        [
            pltpu.make_async_copy(rhs_hbm.at[0], rhs_ref, sems.at[0]),
            pltpu.make_async_copy(inv_hbm.at[0], inv_ref, sems.at[1]),
            pltpu.make_async_copy(list_hbm, list_ref, sems.at[2]),
        ]
    )
    levels, _, slots = list_ref.shape
    per_node = inv_ref.shape[0] // tile
    pool = 2 * GROUP * per_node
    solve_rows(inv_ref, rhs_ref, x_ref, piece_refs, tile)
    note_ref[...] = jnp.zeros_like(note_ref)
    for relative in range(CHIPS):
        for level in range(levels):
            places = places_of(list_ref[level], relative, levels, pool, per_node)
            note_ref[level : level + 1, :slots] = places.astype(jnp.float32)
        noted_refs[relative][:per_node] = piece_refs[relative][...]
        noted_refs[relative][per_node] = note_ref[...].astype(jnp.bfloat16)


def load_kernel(level, after_ref, rhs_hbm, inv_hbm, factor_hbm, rhs_ref, inv_ref, turned_ref, *scratch):
    factor_ref, sems = scratch
    copies = [
        pltpu.make_async_copy(
            factor_hbm.at[level - 1, :, chip_place() ^ relative],
            factor_ref.at[place],
            sems.at[place],
        )
        for place, relative in enumerate(ORDER)
    ] + [
        pltpu.make_async_copy(rhs_hbm.at[level], rhs_ref, sems.at[CHIPS]),
        pltpu.make_async_copy(inv_hbm.at[level], inv_ref, sems.at[CHIPS + 1]),
    ]
    for copy in copies:
        copy.start()
    for relative in range(CHIPS):
        copies[relative].wait()
        slots, quarter, width = factor_ref.shape[1:]
        depth = slots * quarter
        turned_ref[:, relative * depth : (relative + 1) * depth] = (
            factor_ref[relative].reshape(depth, width).T
        )
    for copy in copies[CHIPS:]:
        copy.wait()


def store_kernel(level, x_ref, *refs):
    out_hbm, sem = refs[-2:]
    run_copies([pltpu.make_async_copy(x_ref, out_hbm.at[level], sem)])


def live_part(level, count_ref, part_ref):
    slots, quarter, columns = part_ref.shape
    count = count_ref[:, level - 1 : level]
    part = part_ref[...].reshape(slots * quarter, columns)
    slot_row = lax.broadcasted_iota(jnp.int32, part.shape, 0)
    return jnp.where(slot_row < count * quarter, part, jnp.zeros_like(part))


def less_update(level, relatives, count_ref, base_ref, turned_ref, part_refs, joined_ref, out_ref):
    depth = joined_ref.shape[0] // len(relatives)
    for index, part_ref in enumerate(part_refs):
        joined_ref[index * depth : (index + 1) * depth, :] = live_part(
            level, count_ref, part_ref
        )
    first = ORDER.index(relatives[0]) * depth
    update = jnp.dot(
        turned_ref[:, first : first + joined_ref.shape[0]],
        joined_ref[...],
        preferred_element_type=jnp.float32,
    )
    out_ref[...] = (base_ref[...].astype(jnp.float32) - update).astype(out_ref.dtype)


def update_kernel(level, relatives, count_ref, base_ref, turned_ref, *refs):
    parts, (out_ref, joined_ref) = refs[:-2], refs[-2:]
    less_update(
        level, relatives, count_ref, base_ref, turned_ref, parts, joined_ref, out_ref
    )


def level_kernel(level, levels, tile, relatives, count_ref, base_ref, inv_ref, turned_ref, *refs):
    last = level == levels - 1
    parts, refs = refs[: len(relatives)], refs[len(relatives) :]
    joined_ref, reduced_ref = refs[-2:]
    refs = refs[:-1]
    less_update(
        level, relatives, count_ref, base_ref, turned_ref, parts, joined_ref, reduced_ref
    )
    if not last:
        solve_rows(inv_ref, reduced_ref, refs[0], refs[1:-1], tile)
        return
    out_hbm, x_ref, sems = refs[1:-1]

    def row_copy(i):
        rows = pl.ds(i * tile, tile)
        return pltpu.make_async_copy(x_ref.at[rows], out_hbm.at[level, rows], sems.at[i])

    solve_rows(inv_ref, reduced_ref, x_ref, (), tile, lambda i: row_copy(i).start())
    for i in range(inv_ref.shape[0] // tile):
        row_copy(i).wait()


def select_kernel(level, last, *refs):
    notes, refs = refs[:CHIPS], refs[CHIPS:]
    old, fresh = refs[: level - 1], refs[level - 1 : -CHIPS - 1]
    pool_ref, outs = (refs[-1], refs[-CHIPS - 1 : -1]) if last else (refs[-CHIPS - 1], refs[-CHIPS:])
    step = pool_ref.shape[0] // len(fresh)
    for place, ref in enumerate(fresh):
        pool_ref[place * step : (place + 1) * step] = ref[:step]
    size = pool_ref.shape[0]
    slots = outs[0].shape[0]
    for relative, out_ref in enumerate(outs):
        note = notes[relative][notes[relative].shape[0] - 1].astype(jnp.float32)
        places = note[:, :128].astype(jnp.int32)
        for slot in range(slots):
            place = places[level - 1, slot]
            if level == 1:
                out_ref[slot] = pool_ref[place]
                continue
            value = None
            for index, pool in enumerate(old + (pool_ref,)):
                local = place - index * size
                found = pool[jnp.clip(local, 0, size - 1)]
                value = found if value is None else jnp.where(local >= 0, found, value)
            out_ref[slot] = value


def body(rhs, inv_diag, factor, tile_list, live_count):
    levels, width, columns = rhs.shape
    slots = tile_list.shape[2]
    tile = factor.shape[1] // slots
    per_node = width // tile
    quarter = tile // CHIPS
    pool = 2 * GROUP * per_node
    half = jnp.bfloat16
    piece = jax.ShapeDtypeStruct((per_node, quarter, columns), half)
    solved = jax.ShapeDtypeStruct((width, columns), jnp.float32)
    part = jax.ShapeDtypeStruct((slots, quarter, columns), half)
    out_shape = jax.ShapeDtypeStruct((levels, width, columns), jnp.float32)
    solve_flops = width * width * columns
    part_flops = 2 * slots * quarter * width * columns
    part_moved = 2 * slots * quarter * (width + columns) + 8 * width * columns
    semaphores = pltpu.SemaphoreType.DMA

    rhs, inv_diag, factor, tile_list = (
        pltpu.with_memory_space_constraint(value, pltpu.HBM)
        for value in (
            rhs,
            inv_diag,
            factor.reshape(-1, slots, CHIPS, quarter, width),
            tile_list,
        )
    )

    assert (levels - 1) * pool <= 256 and levels - 1 <= quarter and slots <= columns
    shapes = (solved,) + (piece,) * CHIPS
    noted = jax.ShapeDtypeStruct((per_node + 1, quarter, columns), half)
    solution, *outputs = call(
        functools.partial(first_kernel, tile),
        shapes + (noted,) * CHIPS,
        [HBM] * 3,
        [VMEM] * (len(shapes) + CHIPS),
        solve_flops,
        2 * width * (width + 4 * columns),
        [
            pltpu.VMEM((width, columns), half),
            pltpu.VMEM((width, width), half),
            pltpu.VMEM(tile_list.shape, jnp.int32),
            pltpu.VMEM((quarter, columns), jnp.float32),
            semaphores((3,)),
        ],
    )(tile_list, rhs, inv_diag)
    pieces, noted = outputs[:CHIPS], outputs[CHIPS:]

    own = [noted[0]] + [send(noted[hop], hop) for hop in range(1, CHIPS)]
    notes = own
    counts = live_count.T

    pools = []
    for level in range(1, levels):
        last = level == levels - 1
        previous = [send(pieces[hop], hop, 1) for hop in range(CHIPS)]
        if level > 1:
            own = [pieces[0]] + [send(pieces[hop], hop) for hop in range(1, CHIPS)]
        rhs_here, inv_here, turned = call(
            functools.partial(load_kernel, level),
            (
                jax.ShapeDtypeStruct((width, columns), half),
                jax.ShapeDtypeStruct((width, width), half),
                jax.ShapeDtypeStruct((width, slots * tile), half),
            ),
            [HBM] * 4,
            [VMEM] * 3,
            0,
            2 * width * (columns + width + slots * tile),
            [pltpu.VMEM((CHIPS, slots, quarter, width), half), semaphores((2 + CHIPS,))],
        )(pieces[0], rhs, inv_diag, factor)
        out = call(
            functools.partial(store_kernel, level - 1),
            out_shape,
            [VMEM] if level == 1 else [VMEM, HBM],
            HBM,
            0,
            4 * width * columns,
            [semaphores],
            {} if level == 1 else {1: 0},
        )(*((solution,) if level == 1 else (solution, out)))
        fresh = (
            previous
            + [swap(value) for value in previous]
            + own
            + [swap(value) for value in own]
        )

        inputs = pools + fresh
        packed = jax.ShapeDtypeStruct((pool, quarter, columns), half)
        selected = call(
            functools.partial(select_kernel, level, last),
            (part,) * CHIPS if last else (packed,) + (part,) * CHIPS,
            [VMEM] * (CHIPS + len(inputs)),
            [VMEM] * (CHIPS if last else 1 + CHIPS),
            0,
            4 * (slots * CHIPS + pool) * quarter * columns,
            [pltpu.VMEM(packed.shape, half)] if last else [],
        )(*notes, *inputs)
        pools, parts = pools + list(selected[:-CHIPS]), selected[-CHIPS:]
        parts = [parts[0]] + [send(parts[hop], hop) for hop in range(1, CHIPS)]
        late = LATE
        early = tuple(hop for hop in range(CHIPS) if hop not in late)
        base = call(
            functools.partial(update_kernel, level, early),
            solved,
            [VMEM] * (3 + len(early)),
            VMEM,
            part_flops * len(early),
            part_moved * len(early),
            [pltpu.VMEM((len(early) * slots * quarter, columns), half)],
        )(counts, rhs_here, turned, *[parts[hop] for hop in early])
        level_call = functools.partial(
            call,
            functools.partial(level_kernel, level, levels, tile, late),
            flops=solve_flops + part_flops * len(late),
            moved=part_moved * len(late),
        )
        operands = (counts, base, inv_here, turned) + tuple(parts[hop] for hop in late)
        in_specs = [VMEM] * len(operands)
        joined = pltpu.VMEM((len(late) * slots * quarter, columns), half)
        reduced = pltpu.VMEM((width, columns), half)
        if last:
            return level_call(
                out_shape=out_shape,
                in_specs=in_specs + [HBM],
                out_specs=HBM,
                scratch=[pltpu.VMEM((width, columns), jnp.float32), semaphores((per_node,)), joined, reduced],
                aliases={len(operands): 0},
            )(*operands, out)
        solution, *pieces = level_call(
            out_shape=shapes,
            in_specs=in_specs,
            out_specs=[VMEM] * len(shapes),
            scratch=[joined, reduced],
        )(*operands)


def solution(mesh):
    return jax.shard_map(
        body,
        mesh=mesh,
        in_specs=(
            P(None, "nodes", None),
            P(None, "nodes", None),
            P(None, "nodes", None),
            P(None, "nodes", None),
            P(None, "nodes"),
        ),
        out_specs=P(None, "nodes", None),
        check_vma=False,
    )
```

profile of v0, /device:TPU:0, one launch (start us, length us, event | category | flops | bytes accessed | tf_op | source)
XLA Modules:
  0.0 96.5 jit_solution(17190785560002902861)
XLA Ops:
  0.0 1.6 %shard_map.55 = (f32[640,256]{1,0:T(8,128)S(1)}, bf16[5,32,256]{2,1,0:T(8,128)(2,1)S(1)}, bf16[5,32,256]{2,1,0:T(8,128)(2,1)S(1)}, bf16[5,32,256]{2,1,0:T(8,128)...) custom-call(s32[3,1,12]{2,1,0:T(1,128)} %list_hbm.1, ...), custom_call_target="tpu_custom_call" | custom-call | flops 104857600 | bytes 2129920 | tf_op jit(solution)/shard_map/pallas_call | solution.py:257
  1.6 3.1 %collective-permute-start.3 = (bf16[5,32,256]{2,1,0:T(8,128)(2,1)S(1)}, bf16[5,32,256]{2,1,0:T(8,128)(2,1)S(1)}, u32[]{:S(2)}, u32[]{:S(2)}) collective-permute-start(bf16[5,32,256]{2,1,0:T(8,128)(2,1)S(1)} %get-tuple-element.47.after_ref), channel_id=1, source_target_pairs={{0,8},{1,9},{2,10},{3,11},{4,12},{5,13},{6,14},{7,15},{8,16},{9,17... | collective-permute-start | bytes 245768 | tf_op jit(solution)/shard_map/ppermute | solution.py:28
  4.7 3.5 %collective-permute-start.6 = (bf16[5,32,256]{2,1,0:T(8,128)(2,1)S(1)}, bf16[5,32,256]{2,1,0:T(8,128)(2,1)S(1)}, u32[]{:S(2)}, u32[]{:S(2)}) collective-permute-start(bf16[5,32,256]{2,1,0:T(8,128)(2,1)S(1)} %get-tuple-element.56), channel_id=1, source_target_pairs={{0,14},{1,15},{2,12},{3,13},{4,10},{5,11},{6,8},{7,9},{8,22},{9,23... | collective-permute-start | bytes 245768 | tf_op jit(solution)/shard_map/ppermute | solution.py:28
  8.2 1.5 %collective-permute-start.4 = (bf16[5,32,256]{2,1,0:T(8,128)(2,1)S(1)}, bf16[5,32,256]{2,1,0:T(8,128)(2,1)S(1)}, u32[]{:S(2)}, u32[]{:S(2)}) collective-permute-start(bf16[5,32,256]{2,1,0:T(8,128)(2,1)S(1)} %get-tuple-element.54), channel_id=1, source_target_pairs={{0,10},{1,11},{2,8},{3,9},{4,14},{5,15},{6,12},{7,13},{8,18},{9,19... | collective-permute-start | bytes 245768 | tf_op jit(solution)/shard_map/ppermute | solution.py:28
  13.5 2.7 %collective-permute-start.2 = (bf16[6,32,256]{2,1,0:T(8,128)(2,1)S(1)}, bf16[6,32,256]{2,1,0:T(8,128)(2,1)S(1)}, u32[]{:S(2)}, u32[]{:S(2)}) collective-permute-start(bf16[6,32,256]{2,1,0:T(8,128)(2,1)S(1)} %get-tuple-element.53), channel_id=1, source_target_pairs={{0,6},{1,7},{2,4},{3,5},{4,2},{5,3},{6,0},{7,1},{8,14},{9,15},{10,... | collective-permute-start | bytes 294920 | tf_op jit(solution)/shard_map/ppermute | solution.py:28
  16.2 2.7 %collective-permute-done.5.refs_6_ = bf16[5,32,256]{2,1,0:T(8,128)(2,1)S(1)} collective-permute-done((bf16[5,32,256]{2,1,0:T(8,128)(2,1)S(1)}, bf16[5,32,256]{2,1,0:T(8,128)(2,1)S(1)}, u32[]{:S(2)}, u32[]{:S(2)}) %collective-permute-start.5) | collective-permute-done | bytes 81952 | tf_op jit(solution)/shard_map/ppermute | solution.py:28
  22.8 1.7 %collective-permute-start.16 = (bf16[12,32,256]{2,1,0:T(8,128)(2,1)S(1)}, bf16[12,32,256]{2,1,0:T(8,128)(2,1)S(1)}, u32[]{:S(2)}, u32[]{:S(2)}) collective-permute-start(bf16[12,32,256]{2,1,0:T(8,128)(2,1)S(1)} %get-tuple-element.60), channel_id=1, source_target_pairs={{0,4},{1,5},{2,6},{3,7},{4,0},{5,1},{6,2},{7,3},{8,12},{9,13},{10,... | collective-permute-start | bytes 589832 | tf_op jit(solution)/shard_map/ppermute | solution.py:28
  26.0 1.9 %shard_map.56 = (bf16[640,256]{1,0:T(8,128)(2,1)S(1)}, bf16[640,640]{1,0:T(8,128)(2,1)S(1)}, bf16[640,1536]{1,0:T(8,128)(2,1)S(1)}) custom-call(bf16[5,32,256]{2,1,0:T(8,128)(2,1)S(1)} %get-tuple-element.47.after_ref, bf16[4,640,256]{2,1,0:T(8,128)(2,1)} %rhs_hbm.7, bf16[4,640,640]{2,1,0:T(8,128)(2,1)} %inv_hbm.7, bf16[3,12,4,32,640]{4,3,2,1,0:T(8,128)(2,1)} %bitcast.8), custom_call_target="tpu_custom_call" | custom-call | bytes 3112960 | tf_op jit(solution)/shard_map/pallas_call | solution.py:284
  27.9 2.4 %collective-permute-done.15.refs_1_ = bf16[12,32,256]{2,1,0:T(8,128)(2,1)S(1)} collective-permute-done((bf16[12,32,256]{2,1,0:T(8,128)(2,1)S(1)}, bf16[12,32,256]{2,1,0:T(8,128)(2,1)S(1)}, u32[]{:S(2)}, u32[]{:S(2)}) %collective-permute-start.15) | collective-permute-done | bytes 196640 | tf_op jit(solution)/shard_map/ppermute | solution.py:28
  30.8 2.4 %collective-permute-done.16.refs_0_ = bf16[12,32,256]{2,1,0:T(8,128)(2,1)S(1)} collective-permute-done((bf16[12,32,256]{2,1,0:T(8,128)(2,1)S(1)}, bf16[12,32,256]{2,1,0:T(8,128)(2,1)S(1)}, u32[]{:S(2)}, u32[]{:S(2)}) %collective-permute-start.16) | collective-permute-done | bytes 196640 | tf_op jit(solution)/shard_map/ppermute | solution.py:28
  35.5 2.1 %collective-permute-start.19 = (bf16[5,32,256]{2,1,0:T(8,128)(2,1)S(1)}, bf16[5,32,256]{2,1,0:T(8,128)(2,1)S(1)}, u32[]{:S(2)}, u32[]{:S(2)}) collective-permute-start(bf16[5,32,256]{2,1,0:T(8,128)(2,1)S(1)} %get-tuple-element.66), channel_id=1, source_target_pairs={{0,10},{1,11},{2,8},{3,9},{4,14},{5,15},{6,12},{7,13},{8,18},{9,19... | collective-permute-start | bytes 245768 | tf_op jit(solution)/shard_map/ppermute | solution.py:28
  37.6 1.6 %collective-permute-start.20 = (bf16[5,32,256]{2,1,0:T(8,128)(2,1)S(1)}, bf16[5,32,256]{2,1,0:T(8,128)(2,1)S(1)}, u32[]{:S(2)}, u32[]{:S(2)}) collective-permute-start(bf16[5,32,256]{2,1,0:T(8,128)(2,1)S(1)} %get-tuple-element.67), channel_id=1, source_target_pairs={{0,12},{1,13},{2,14},{3,15},{4,8},{5,9},{6,10},{7,11},{8,20},{9,21... | collective-permute-start | bytes 245768 | tf_op jit(solution)/shard_map/ppermute | solution.py:28
  39.2 2.8 %collective-permute-start.21 = (bf16[5,32,256]{2,1,0:T(8,128)(2,1)S(1)}, bf16[5,32,256]{2,1,0:T(8,128)(2,1)S(1)}, u32[]{:S(2)}, u32[]{:S(2)}) collective-permute-start(bf16[5,32,256]{2,1,0:T(8,128)(2,1)S(1)} %get-tuple-element.68), channel_id=1, source_target_pairs={{0,14},{1,15},{2,12},{3,13},{4,10},{5,11},{6,8},{7,9},{8,22},{9,23... | collective-permute-start | bytes 245768 | tf_op jit(solution)/shard_map/ppermute | solution.py:28
  54.2 2.0 %collective-permute-start.35 = (bf16[12,32,256]{2,1,0:T(8,128)(2,1)S(1)}, bf16[12,32,256]{2,1,0:T(8,128)(2,1)S(1)}, u32[]{:S(2)}, u32[]{:S(2)}) collective-permute-start(bf16[12,32,256]{2,1,0:T(8,128)(2,1)S(1)} %get-tuple-element.73), channel_id=1, source_target_pairs={{0,6},{1,7},{2,4},{3,5},{4,2},{5,3},{6,0},{7,1},{8,14},{9,15},{10,... | collective-permute-start | bytes 589832 | tf_op jit(solution)/shard_map/ppermute | solution.py:28
  56.2 1.9 %shard_map.60 = (bf16[640,256]{1,0:T(8,128)(2,1)S(1)}, bf16[640,640]{1,0:T(8,128)(2,1)S(1)}, bf16[640,1536]{1,0:T(8,128)(2,1)S(1)}) custom-call(bf16[5,32,256]{2,1,0:T(8,128)(2,1)S(1)} %get-tuple-element.62.after_ref.refs_13_, bf16[4,640,256]{2,1,0:T(8,128)(2,1)} %rhs_hbm.7, bf16[4,640,640]{2,1,0:T(8,128)(2,1)} %inv_hbm.7, bf16[3,12,4,32,640]{4,3,2,1,0:T(8,128)(2,1)} %bitcast.9), custom_call_target="tpu_custom_call" | custom-call | bytes 3112960 | tf_op jit(solution)/shard_map/pallas_call | solution.py:284
  58.1 2.4 %collective-permute-done.33.refs_1_ = bf16[12,32,256]{2,1,0:T(8,128)(2,1)S(1)} collective-permute-done((bf16[12,32,256]{2,1,0:T(8,128)(2,1)S(1)}, bf16[12,32,256]{2,1,0:T(8,128)(2,1)S(1)}, u32[]{:S(2)}, u32[]{:S(2)}) %collective-permute-start.33) | collective-permute-done | bytes 196640 | tf_op jit(solution)/shard_map/ppermute | solution.py:28
  61.0 3.4 %collective-permute-done.34.refs_0_ = bf16[12,32,256]{2,1,0:T(8,128)(2,1)S(1)} collective-permute-done((bf16[12,32,256]{2,1,0:T(8,128)(2,1)S(1)}, bf16[12,32,256]{2,1,0:T(8,128)(2,1)S(1)}, u32[]{:S(2)}, u32[]{:S(2)}) %collective-permute-start.34) | collective-permute-done | bytes 196640 | tf_op jit(solution)/shard_map/ppermute | solution.py:28
  65.7 1.6 %collective-permute-start.37 = (bf16[5,32,256]{2,1,0:T(8,128)(2,1)S(1)}, bf16[5,32,256]{2,1,0:T(8,128)(2,1)S(1)}, u32[]{:S(2)}, u32[]{:S(2)}) collective-permute-start(bf16[5,32,256]{2,1,0:T(8,128)(2,1)S(1)} %get-tuple-element.78), channel_id=1, source_target_pairs={{0,10},{1,11},{2,8},{3,9},{4,14},{5,15},{6,12},{7,13},{8,18},{9,19... | collective-permute-start | bytes 245768 | tf_op jit(solution)/shard_map/ppermute | solution.py:28
  67.3 2.1 %collective-permute-start.38 = (bf16[5,32,256]{2,1,0:T(8,128)(2,1)S(1)}, bf16[5,32,256]{2,1,0:T(8,128)(2,1)S(1)}, u32[]{:S(2)}, u32[]{:S(2)}) collective-permute-start(bf16[5,32,256]{2,1,0:T(8,128)(2,1)S(1)} %get-tuple-element.79), channel_id=1, source_target_pairs={{0,12},{1,13},{2,14},{3,15},{4,8},{5,9},{6,10},{7,11},{8,20},{9,21... | collective-permute-start | bytes 245768 | tf_op jit(solution)/shard_map/ppermute | solution.py:28
  69.4 2.9 %collective-permute-start.39 = (bf16[5,32,256]{2,1,0:T(8,128)(2,1)S(1)}, bf16[5,32,256]{2,1,0:T(8,128)(2,1)S(1)}, u32[]{:S(2)}, u32[]{:S(2)}) collective-permute-start(bf16[5,32,256]{2,1,0:T(8,128)(2,1)S(1)} %get-tuple-element.80), channel_id=1, source_target_pairs={{0,14},{1,15},{2,12},{3,13},{4,10},{5,11},{6,8},{7,9},{8,22},{9,23... | collective-permute-start | bytes 245768 | tf_op jit(solution)/shard_map/ppermute | solution.py:28
  74.9 1.6 %collective-permute-start.46 = (bf16[5,32,256]{2,1,0:T(8,128)(2,1)S(1)}, bf16[5,32,256]{2,1,0:T(8,128)(2,1)S(1)}, u32[]{:S(2)}, u32[]{:S(2)}) collective-permute-start(bf16[5,32,256]{2,1,0:T(8,128)(2,1)S(1)} %get-tuple-element.80), channel_id=1, source_target_pairs={{0,6},{1,7},{2,4},{3,5},{4,2},{5,3},{6,0},{7,1},{8,14},{9,15},{10,... | collective-permute-start | bytes 245768 | tf_op jit(solution)/shard_map/ppermute | solution.py:28
  88.0 1.9 %shard_map.64 = (bf16[640,256]{1,0:T(8,128)(2,1)S(1)}, bf16[640,640]{1,0:T(8,128)(2,1)S(1)}, bf16[640,1536]{1,0:T(8,128)(2,1)S(1)}) custom-call(bf16[5,32,256]{2,1,0:T(8,128)(2,1)S(1)} %get-tuple-element.74.after_ref.refs_14_, bf16[4,640,256]{2,1,0:T(8,128)(2,1)} %rhs_hbm.7, bf16[4,640,640]{2,1,0:T(8,128)(2,1)} %inv_hbm.7, bf16[3,12,4,32,640]{4,3,2,1,0:T(8,128)(2,1)} %bitcast.10), custom_call_target="tpu_custom_call" | custom-call | bytes 3112960 | tf_op jit(solution)/shard_map/pallas_call | solution.py:284
  91.3 3.5 %collective-permute-done.52.refs_0_ = bf16[12,32,256]{2,1,0:T(8,128)(2,1)S(1)} collective-permute-done((bf16[12,32,256]{2,1,0:T(8,128)(2,1)S(1)}, bf16[12,32,256]{2,1,0:T(8,128)(2,1)S(1)}, u32[]{:S(2)}, u32[]{:S(2)}) %collective-permute-start.52) | collective-permute-done | bytes 196640 | tf_op jit(solution)/shard_map/ppermute | solution.py:28
  94.8 1.8 %shard_map.70 = f32[4,640,256]{2,1,0:T(8,128)} custom-call(s32[1,3]{1,0:T(1,128)S(1)} %bitcast.7, f32[640,256]{1,0:T(8,128)S(1)} %shard_map.66.base_ref, bf16[640,640]{1,0:T(8,128)(2,1)S(1)} %get-tuple-element.83.inv_ref, bf16[640,1536]{1,0:T(8,128)(2,1)S(1)} %get-tuple-element.76.turned_ref, ...), custom_call_target="tpu_custom_call", output_to_operand_aliasing={{}: (6, {})} | custom-call | flops 356515840 | bytes 3997696 | tf_op jit(solution)/shard_map/pallas_call | solution.py:349
  (102 shorter events, 41.3 us)
Async XLA Ops:
  1.6 9.8 %collective-permute-start.3 = (bf16[5,32,256]{2,1,0:T(8,128)(2,1)S(1)}, bf16[5,32,256]{2,1,0:T(8,128)(2,1)S(1)}, u32[]{:S(2)}, u32[]{:S(2)}) collective-permute-start(bf16[5,32,256]{2,1,0:T(8,128)(2,1)S(1)} %get-tuple-element.47.after_ref), channel_id=1, source_target_pairs={{0,8},{1,9},{2,10},{3,11},{4,12},{5,13},{6,14},{7,15},{8,16},{9,17... | collective-permute-start | bytes 245768 | tf_op jit(solution)/shard_map/ppermute | solution.py:28
  4.7 8.7 %collective-permute-start.6 = (bf16[5,32,256]{2,1,0:T(8,128)(2,1)S(1)}, bf16[5,32,256]{2,1,0:T(8,128)(2,1)S(1)}, u32[]{:S(2)}, u32[]{:S(2)}) collective-permute-start(bf16[5,32,256]{2,1,0:T(8,128)(2,1)S(1)} %get-tuple-element.56), channel_id=1, source_target_pairs={{0,14},{1,15},{2,12},{3,13},{4,10},{5,11},{6,8},{7,9},{8,22},{9,23... | collective-permute-start | bytes 245768 | tf_op jit(solution)/shard_map/ppermute | solution.py:28
  8.2 8.0 %collective-permute-start.4 = (bf16[5,32,256]{2,1,0:T(8,128)(2,1)S(1)}, bf16[5,32,256]{2,1,0:T(8,128)(2,1)S(1)}, u32[]{:S(2)}, u32[]{:S(2)}) collective-permute-start(bf16[5,32,256]{2,1,0:T(8,128)(2,1)S(1)} %get-tuple-element.54), channel_id=1, source_target_pairs={{0,10},{1,11},{2,8},{3,9},{4,14},{5,15},{6,12},{7,13},{8,18},{9,19... | collective-permute-start | bytes 245768 | tf_op jit(solution)/shard_map/ppermute | solution.py:28
  9.7 9.1 %collective-permute-start = (bf16[6,32,256]{2,1,0:T(8,128)(2,1)S(1)}, bf16[6,32,256]{2,1,0:T(8,128)(2,1)S(1)}, u32[]{:S(2)}, u32[]{:S(2)}) collective-permute-start(bf16[6,32,256]{2,1,0:T(8,128)(2,1)S(1)} %get-tuple-element.51), channel_id=1, source_target_pairs={{0,2},{1,3},{2,0},{3,1},{4,6},{5,7},{6,4},{7,5},{8,10},{9,11},{10,... | collective-permute-start | bytes 294920 | tf_op jit(solution)/shard_map/ppermute | solution.py:28
  11.2 7.6 %collective-permute-start.5 = (bf16[5,32,256]{2,1,0:T(8,128)(2,1)S(1)}, bf16[5,32,256]{2,1,0:T(8,128)(2,1)S(1)}, u32[]{:S(2)}, u32[]{:S(2)}) collective-permute-start(bf16[5,32,256]{2,1,0:T(8,128)(2,1)S(1)} %get-tuple-element.55), channel_id=1, source_target_pairs={{0,12},{1,13},{2,14},{3,15},{4,8},{5,9},{6,10},{7,11},{8,20},{9,21... | collective-permute-start | bytes 245768 | tf_op jit(solution)/shard_map/ppermute | solution.py:28
  11.4 8.5 %collective-permute-start.1 = (bf16[6,32,256]{2,1,0:T(8,128)(2,1)S(1)}, bf16[6,32,256]{2,1,0:T(8,128)(2,1)S(1)}, u32[]{:S(2)}, u32[]{:S(2)}) collective-permute-start(bf16[6,32,256]{2,1,0:T(8,128)(2,1)S(1)} %get-tuple-element.52), channel_id=1, source_target_pairs={{0,4},{1,5},{2,6},{3,7},{4,0},{5,1},{6,2},{7,3},{8,12},{9,13},{10,... | collective-permute-start | bytes 294920 | tf_op jit(solution)/shard_map/ppermute | solution.py:28
  13.5 6.4 %collective-permute-start.2 = (bf16[6,32,256]{2,1,0:T(8,128)(2,1)S(1)}, bf16[6,32,256]{2,1,0:T(8,128)(2,1)S(1)}, u32[]{:S(2)}, u32[]{:S(2)}) collective-permute-start(bf16[6,32,256]{2,1,0:T(8,128)(2,1)S(1)} %get-tuple-element.53), channel_id=1, source_target_pairs={{0,6},{1,7},{2,4},{3,5},{4,2},{5,3},{6,0},{7,1},{8,14},{9,15},{10,... | collective-permute-start | bytes 294920 | tf_op jit(solution)/shard_map/ppermute | solution.py:28
  22.4 7.8 %collective-permute-start.15 = (bf16[12,32,256]{2,1,0:T(8,128)(2,1)S(1)}, bf16[12,32,256]{2,1,0:T(8,128)(2,1)S(1)}, u32[]{:S(2)}, u32[]{:S(2)}) collective-permute-start(bf16[12,32,256]{2,1,0:T(8,128)(2,1)S(1)} %get-tuple-element.58), channel_id=1, source_target_pairs={{0,2},{1,3},{2,0},{3,1},{4,6},{5,7},{6,4},{7,5},{8,10},{9,11},{10,... | collective-permute-start | bytes 589832 | tf_op jit(solution)/shard_map/ppermute | solution.py:28
  22.8 10.4 %collective-permute-start.16 = (bf16[12,32,256]{2,1,0:T(8,128)(2,1)S(1)}, bf16[12,32,256]{2,1,0:T(8,128)(2,1)S(1)}, u32[]{:S(2)}, u32[]{:S(2)}) collective-permute-start(bf16[12,32,256]{2,1,0:T(8,128)(2,1)S(1)} %get-tuple-element.60), channel_id=1, source_target_pairs={{0,4},{1,5},{2,6},{3,7},{4,0},{5,1},{6,2},{7,3},{8,12},{9,13},{10,... | collective-permute-start | bytes 589832 | tf_op jit(solution)/shard_map/ppermute | solution.py:28
  24.5 9.5 %collective-permute-start.17 = (bf16[12,32,256]{2,1,0:T(8,128)(2,1)S(1)}, bf16[12,32,256]{2,1,0:T(8,128)(2,1)S(1)}, u32[]{:S(2)}, u32[]{:S(2)}) collective-permute-start(bf16[12,32,256]{2,1,0:T(8,128)(2,1)S(1)} %get-tuple-element.61), channel_id=1, source_target_pairs={{0,6},{1,7},{2,4},{3,5},{4,2},{5,3},{6,0},{7,1},{8,14},{9,15},{10,... | collective-permute-start | bytes 589832 | tf_op jit(solution)/shard_map/ppermute | solution.py:28
  35.2 8.2 %collective-permute-start.18 = (bf16[5,32,256]{2,1,0:T(8,128)(2,1)S(1)}, bf16[5,32,256]{2,1,0:T(8,128)(2,1)S(1)}, u32[]{:S(2)}, u32[]{:S(2)}) collective-permute-start(bf16[5,32,256]{2,1,0:T(8,128)(2,1)S(1)} %get-tuple-element.62.after_ref.refs_13_), channel_id=1, source_target_pairs={{0,8},{1,9},{2,10},{3,11},{4,12},{5,13},{6,14},{7,15},{8,16},{9,17... | collective-permute-start | bytes 245768 | tf_op jit(solution)/shard_map/ppermute | solution.py:28
  35.5 9.5 %collective-permute-start.19 = (bf16[5,32,256]{2,1,0:T(8,128)(2,1)S(1)}, bf16[5,32,256]{2,1,0:T(8,128)(2,1)S(1)}, u32[]{:S(2)}, u32[]{:S(2)}) collective-permute-start(bf16[5,32,256]{2,1,0:T(8,128)(2,1)S(1)} %get-tuple-element.66), channel_id=1, source_target_pairs={{0,10},{1,11},{2,8},{3,9},{4,14},{5,15},{6,12},{7,13},{8,18},{9,19... | collective-permute-start | bytes 245768 | tf_op jit(solution)/shard_map/ppermute | solution.py:28
  37.6 8.4 %collective-permute-start.20 = (bf16[5,32,256]{2,1,0:T(8,128)(2,1)S(1)}, bf16[5,32,256]{2,1,0:T(8,128)(2,1)S(1)}, u32[]{:S(2)}, u32[]{:S(2)}) collective-permute-start(bf16[5,32,256]{2,1,0:T(8,128)(2,1)S(1)} %get-tuple-element.67), channel_id=1, source_target_pairs={{0,12},{1,13},{2,14},{3,15},{4,8},{5,9},{6,10},{7,11},{8,20},{9,21... | collective-permute-start | bytes 245768 | tf_op jit(solution)/shard_map/ppermute | solution.py:28
  39.2 8.2 %collective-permute-start.21 = (bf16[5,32,256]{2,1,0:T(8,128)(2,1)S(1)}, bf16[5,32,256]{2,1,0:T(8,128)(2,1)S(1)}, u32[]{:S(2)}, u32[]{:S(2)}) collective-permute-start(bf16[5,32,256]{2,1,0:T(8,128)(2,1)S(1)} %get-tuple-element.68), channel_id=1, source_target_pairs={{0,14},{1,15},{2,12},{3,13},{4,10},{5,11},{6,8},{7,9},{8,22},{9,23... | collective-permute-start | bytes 245768 | tf_op jit(solution)/shard_map/ppermute | solution.py:28
  52.7 7.8 %collective-permute-start.33 = (bf16[12,32,256]{2,1,0:T(8,128)(2,1)S(1)}, bf16[12,32,256]{2,1,0:T(8,128)(2,1)S(1)}, u32[]{:S(2)}, u32[]{:S(2)}) collective-permute-start(bf16[12,32,256]{2,1,0:T(8,128)(2,1)S(1)} %get-tuple-element.70), channel_id=1, source_target_pairs={{0,2},{1,3},{2,0},{3,1},{4,6},{5,7},{6,4},{7,5},{8,10},{9,11},{10,... | collective-permute-start | bytes 589832 | tf_op jit(solution)/shard_map/ppermute | solution.py:28
  53.3 11.1 %collective-permute-start.34 = (bf16[12,32,256]{2,1,0:T(8,128)(2,1)S(1)}, bf16[12,32,256]{2,1,0:T(8,128)(2,1)S(1)}, u32[]{:S(2)}, u32[]{:S(2)}) collective-permute-start(bf16[12,32,256]{2,1,0:T(8,128)(2,1)S(1)} %get-tuple-element.72), channel_id=1, source_target_pairs={{0,4},{1,5},{2,6},{3,7},{4,0},{5,1},{6,2},{7,3},{8,12},{9,13},{10,... | collective-permute-start | bytes 589832 | tf_op jit(solution)/shard_map/ppermute | solution.py:28
  54.2 10.2 %collective-permute-start.35 = (bf16[12,32,256]{2,1,0:T(8,128)(2,1)S(1)}, bf16[12,32,256]{2,1,0:T(8,128)(2,1)S(1)}, u32[]{:S(2)}, u32[]{:S(2)}) collective-permute-start(bf16[12,32,256]{2,1,0:T(8,128)(2,1)S(1)} %get-tuple-element.73), channel_id=1, source_target_pairs={{0,6},{1,7},{2,4},{3,5},{4,2},{5,3},{6,0},{7,1},{8,14},{9,15},{10,... | collective-permute-start | bytes 589832 | tf_op jit(solution)/shard_map/ppermute | solution.py:28
  65.5 8.2 %collective-permute-start.36 = (bf16[5,32,256]{2,1,0:T(8,128)(2,1)S(1)}, bf16[5,32,256]{2,1,0:T(8,128)(2,1)S(1)}, u32[]{:S(2)}, u32[]{:S(2)}) collective-permute-start(bf16[5,32,256]{2,1,0:T(8,128)(2,1)S(1)} %get-tuple-element.74.after_ref.refs_14_), channel_id=1, source_target_pairs={{0,8},{1,9},{2,10},{3,11},{4,12},{5,13},{6,14},{7,15},{8,16},{9,17... | collective-permute-start | bytes 245768 | tf_op jit(solution)/shard_map/ppermute | solution.py:28
  65.7 9.2 %collective-permute-start.37 = (bf16[5,32,256]{2,1,0:T(8,128)(2,1)S(1)}, bf16[5,32,256]{2,1,0:T(8,128)(2,1)S(1)}, u32[]{:S(2)}, u32[]{:S(2)}) collective-permute-start(bf16[5,32,256]{2,1,0:T(8,128)(2,1)S(1)} %get-tuple-element.78), channel_id=1, source_target_pairs={{0,10},{1,11},{2,8},{3,9},{4,14},{5,15},{6,12},{7,13},{8,18},{9,19... | collective-permute-start | bytes 245768 | tf_op jit(solution)/shard_map/ppermute | solution.py:28
  67.3 9.3 %collective-permute-start.38 = (bf16[5,32,256]{2,1,0:T(8,128)(2,1)S(1)}, bf16[5,32,256]{2,1,0:T(8,128)(2,1)S(1)}, u32[]{:S(2)}, u32[]{:S(2)}) collective-permute-start(bf16[5,32,256]{2,1,0:T(8,128)(2,1)S(1)} %get-tuple-element.79), channel_id=1, source_target_pairs={{0,12},{1,13},{2,14},{3,15},{4,8},{5,9},{6,10},{7,11},{8,20},{9,21... | collective-permute-start | bytes 245768 | tf_op jit(solution)/shard_map/ppermute | solution.py:28
  69.4 8.1 %collective-permute-start.39 = (bf16[5,32,256]{2,1,0:T(8,128)(2,1)S(1)}, bf16[5,32,256]{2,1,0:T(8,128)(2,1)S(1)}, u32[]{:S(2)}, u32[]{:S(2)}) collective-permute-start(bf16[5,32,256]{2,1,0:T(8,128)(2,1)S(1)} %get-tuple-element.80), channel_id=1, source_target_pairs={{0,14},{1,15},{2,12},{3,13},{4,10},{5,11},{6,8},{7,9},{8,22},{9,23... | collective-permute-start | bytes 245768 | tf_op jit(solution)/shard_map/ppermute | solution.py:28
  82.7 8.0 %collective-permute-start.51 = (bf16[12,32,256]{2,1,0:T(8,128)(2,1)S(1)}, bf16[12,32,256]{2,1,0:T(8,128)(2,1)S(1)}, u32[]{:S(2)}, u32[]{:S(2)}) collective-permute-start(bf16[12,32,256]{2,1,0:T(8,128)(2,1)S(1)} %get-tuple-element.82), channel_id=1, source_target_pairs={{0,2},{1,3},{2,0},{3,1},{4,6},{5,7},{6,4},{7,5},{8,10},{9,11},{10,... | collective-permute-start | bytes 589832 | tf_op jit(solution)/shard_map/ppermute | solution.py:28
  83.7 11.1 %collective-permute-start.52 = (bf16[12,32,256]{2,1,0:T(8,128)(2,1)S(1)}, bf16[12,32,256]{2,1,0:T(8,128)(2,1)S(1)}, u32[]{:S(2)}, u32[]{:S(2)}) collective-permute-start(bf16[12,32,256]{2,1,0:T(8,128)(2,1)S(1)} %get-tuple-element.84), channel_id=1, source_target_pairs={{0,4},{1,5},{2,6},{3,7},{4,0},{5,1},{6,2},{7,3},{8,12},{9,13},{10,... | collective-permute-start | bytes 589832 | tf_op jit(solution)/shard_map/ppermute | solution.py:28
  85.0 9.8 %collective-permute-start.53 = (bf16[12,32,256]{2,1,0:T(8,128)(2,1)S(1)}, bf16[12,32,256]{2,1,0:T(8,128)(2,1)S(1)}, u32[]{:S(2)}, u32[]{:S(2)}) collective-permute-start(bf16[12,32,256]{2,1,0:T(8,128)(2,1)S(1)} %get-tuple-element.85), channel_id=1, source_target_pairs={{0,6},{1,7},{2,4},{3,5},{4,2},{5,3},{6,0},{7,1},{8,14},{9,15},{10,... | collective-permute-start | bytes 589832 | tf_op jit(solution)/shard_map/ppermute | solution.py:28
  (31 other events, 90.5 us)
where the time goes:
time: 96.8 us; the launch traced here: 96.5 us
  starting transfers between devices  48.9 us (51%)
  waiting for transfers between devices  31 us (32%)
  Pallas kernels  16.4 us (17%)
    ppermute x30, starting transfers between devices, send(): return lax.ppermute(value, 'nodes', route)  45.3 us
    ppermute x30, waiting for transfers between devices, send(): return lax.ppermute(value, 'nodes', route)  27.9 us
    pallas_call x3, Pallas kernels, body(): call(functools.partial(load_kernel, level), (jax.ShapeDtypeStruct((width,...  5.7 us
    ppermute x24, starting transfers between devices, swap(): return lax.ppermute(value, 'nodes', [(i, i ^ 1) for i in range(size)])  3.67 us
    ppermute x24, waiting for transfers between devices, swap(): return lax.ppermute(value, 'nodes', [(i, i ^ 1) for i in range(size)])  3.08 us
    pallas_call x3, Pallas kernels, body(): call(functools.partial(store_kernel, level - 1), out_shape, [VMEM] if lev...  2.54 us
    pallas_call x2, Pallas kernels, body(): level_call(out_shape=shapes, in_specs=in_specs, out_specs=[VMEM] * len(sh...  2.19 us
  transfers between devices with their start and end apart: 54, of which 29 were waited for; matrix products, arithmetic and copies ran while one was open for 0% of the time, Pallas kernels for 10%

commit v1 on v0

--- a/solution.py
+++ b/solution.py
@@ -199,29 +199,19 @@
         row_copy(i).wait()
 
 
-def select_kernel(level, last, *refs):
-    notes, refs = refs[:CHIPS], refs[CHIPS:]
-    old, fresh = refs[: level - 1], refs[level - 1 : -CHIPS - 1]
-    pool_ref, outs = (refs[-1], refs[-CHIPS - 1 : -1]) if last else (refs[-CHIPS - 1], refs[-CHIPS:])
-    step = pool_ref.shape[0] // len(fresh)
+def select_kernel(level, pool, *refs):
+    notes, refs = refs[:CHIPS], refs[CHIPS + (level > 1) :]
+    fresh, pool_ref, outs = refs[: -CHIPS - 1], refs[-CHIPS - 1], refs[-CHIPS:]
+    step = pool // len(fresh)
     for place, ref in enumerate(fresh):
-        pool_ref[place * step : (place + 1) * step] = ref[:step]
-    size = pool_ref.shape[0]
+        first = (level - 1) * pool + place * step
+        pool_ref[first : first + step] = ref[:step]
     slots = outs[0].shape[0]
     for relative, out_ref in enumerate(outs):
         note = notes[relative][notes[relative].shape[0] - 1].astype(jnp.float32)
         places = note[:, :128].astype(jnp.int32)
         for slot in range(slots):
-            place = places[level - 1, slot]
-            if level == 1:
-                out_ref[slot] = pool_ref[place]
-                continue
-            value = None
-            for index, pool in enumerate(old + (pool_ref,)):
-                local = place - index * size
-                found = pool[jnp.clip(local, 0, size - 1)]
-                value = found if value is None else jnp.where(local >= 0, found, value)
-            out_ref[slot] = value
+            out_ref[slot] = pool_ref[places[level - 1, slot]]
 
 
 def body(rhs, inv_diag, factor, tile_list, live_count):
@@ -312,17 +302,17 @@
         )
 
         inputs = pools + fresh
-        packed = jax.ShapeDtypeStruct((pool, quarter, columns), half)
-        selected = call(
-            functools.partial(select_kernel, level, last),
-            (part,) * CHIPS if last else (packed,) + (part,) * CHIPS,
+        packed = jax.ShapeDtypeStruct(((levels - 1) * pool, quarter, columns), half)
+        packed, *parts = call(
+            functools.partial(select_kernel, level, pool),
+            (packed,) + (part,) * CHIPS,
             [VMEM] * (CHIPS + len(inputs)),
-            [VMEM] * (CHIPS if last else 1 + CHIPS),
+            [VMEM] * (1 + CHIPS),
             0,
             4 * (slots * CHIPS + pool) * quarter * columns,
-            [pltpu.VMEM(packed.shape, half)] if last else [],
+            aliases={CHIPS: 0} if pools else {},
         )(*notes, *inputs)
-        pools, parts = pools + list(selected[:-CHIPS]), selected[-CHIPS:]
+        pools = [packed]
         parts = [parts[0]] + [send(parts[hop], hop) for hop in range(1, CHIPS)]
         late = LATE
         early = tuple(hop for hop in range(CHIPS) if hop not in late)

time: 96.8 us -> 99.8 us (1.031)
  waiting for transfers between devices: 31 us -> 33.2 us
  starting transfers between devices: 48.9 us -> 50.1 us
    ppermute x30, waiting for transfers between devices: 27.9 us -> 29.6 us  [send(): return lax.ppermute(value, 'nodes', route)]
    ppermute x24, starting transfers between devices: 3.67 us -> 4.81 us  [swap(): return lax.ppermute(value, 'nodes', [(i, i ^ 1) for i in range(size)])]
  transfers between devices with their start and end apart: 54 -> 54, of which waited for: 29 -> 23; matrix products, arithmetic and copies ran while one was open for 0% -> 0% of each run, Pallas kernels for 10% -> 10%
where the time goes in v1:
time: 99.8 us; the launch traced here: 99.5 us
  starting transfers between devices  50.1 us (50%)
  waiting for transfers between devices  33.2 us (33%)
  Pallas kernels  16 us (16%)
    ppermute x30, starting transfers between devices, send(): return lax.ppermute(value, 'nodes', route)  45.3 us
    ppermute x30, waiting for transfers between devices, send(): return lax.ppermute(value, 'nodes', route)  29.6 us
    pallas_call x3, Pallas kernels, body(): call(functools.partial(load_kernel, level), (jax.ShapeDtypeStruct((width,...  5.7 us
    ppermute x24, starting transfers between devices, swap(): return lax.ppermute(value, 'nodes', [(i, i ^ 1) for i in range(size)])  4.81 us
    ppermute x24, waiting for transfers between devices, swap(): return lax.ppermute(value, 'nodes', [(i, i ^ 1) for i in range(size)])  3.65 us
    pallas_call x3, Pallas kernels, body(): call(functools.partial(store_kernel, level - 1), out_shape, [VMEM] if lev...  2.54 us
    pallas_call x2, Pallas kernels, body(): level_call(out_shape=shapes, in_specs=in_specs, out_specs=[VMEM] * len(sh...  2.19 us
  transfers between devices with their start and end apart: 54, of which 23 were waited for; matrix products, arithmetic and copies ran while one was open for 0% of the time, Pallas kernels for 10%

profile of v1, /device:TPU:0, one launch (start us, length us, event | category | flops | bytes accessed | tf_op | source)
XLA Modules:
  0.0 99.5 jit_solution(3758252970075084657)
XLA Ops:
  1.6 4.0 %collective-permute-start.4 = (bf16[5,32,256]{2,1,0:T(8,128)(2,1)S(1)}, bf16[5,32,256]{2,1,0:T(8,128)(2,1)S(1)}, u32[]{:S(2)}, u32[]{:S(2)}) collective-permute-start(bf16[5,32,256]{2,1,0:T(8,128)(2,1)S(1)} %get-tuple-element.54), channel_id=1, source_target_pairs={{0,10},{1,11},{2,8},{3,9},{4,14},{5,15},{6,12},{7,13},{8,18},{9,19... | collective-permute-start | bytes 245768 | tf_op jit(solution)/shard_map/ppermute | solution.py:28
  5.7 2.5 %collective-permute-start.5 = (bf16[5,32,256]{2,1,0:T(8,128)(2,1)S(1)}, bf16[5,32,256]{2,1,0:T(8,128)(2,1)S(1)}, u32[]{:S(2)}, u32[]{:S(2)}) collective-permute-start(bf16[5,32,256]{2,1,0:T(8,128)(2,1)S(1)} %get-tuple-element.55), channel_id=1, source_target_pairs={{0,12},{1,13},{2,14},{3,15},{4,8},{5,9},{6,10},{7,11},{8,20},{9,21... | collective-permute-start | bytes 245768 | tf_op jit(solution)/shard_map/ppermute | solution.py:28
  14.6 2.6 %collective-permute-done.6.refs_7_ = bf16[5,32,256]{2,1,0:T(8,128)(2,1)S(1)} collective-permute-done((bf16[5,32,256]{2,1,0:T(8,128)(2,1)S(1)}, bf16[5,32,256]{2,1,0:T(8,128)(2,1)S(1)}, u32[]{:S(2)}, u32[]{:S(2)}) %collective-permute-start.6) | collective-permute-done | bytes 81952 | tf_op jit(solution)/shard_map/ppermute | solution.py:28
  23.4 1.7 %collective-permute-start.17 = (bf16[12,32,256]{2,1,0:T(8,128)(2,1)S(1)}, bf16[12,32,256]{2,1,0:T(8,128)(2,1)S(1)}, u32[]{:S(2)}, u32[]{:S(2)}) collective-permute-start(bf16[12,32,256]{2,1,0:T(8,128)(2,1)S(1)} %get-tuple-element.61), channel_id=1, source_target_pairs={{0,6},{1,7},{2,4},{3,5},{4,2},{5,3},{6,0},{7,1},{8,14},{9,15},{10,... | collective-permute-start | bytes 589832 | tf_op jit(solution)/shard_map/ppermute | solution.py:28
  25.1 1.9 %shard_map.56 = (bf16[640,256]{1,0:T(8,128)(2,1)S(1)}, bf16[640,640]{1,0:T(8,128)(2,1)S(1)}, bf16[640,1536]{1,0:T(8,128)(2,1)S(1)}) custom-call(bf16[5,32,256]{2,1,0:T(8,128)(2,1)S(1)} %get-tuple-element.47.after_ref, bf16[4,640,256]{2,1,0:T(8,128)(2,1)} %rhs_hbm.7, bf16[4,640,640]{2,1,0:T(8,128)(2,1)} %inv_hbm.7, bf16[3,12,4,32,640]{4,3,2,1,0:T(8,128)(2,1)} %bitcast.8), custom_call_target="tpu_custom_call" | custom-call | bytes 3112960 | tf_op jit(solution)/shard_map/pallas_call | solution.py:274
  27.0 2.4 %collective-permute-done.15.refs_1_ = bf16[12,32,256]{2,1,0:T(8,128)(2,1)S(1)} collective-permute-done((bf16[12,32,256]{2,1,0:T(8,128)(2,1)S(1)}, bf16[12,32,256]{2,1,0:T(8,128)(2,1)S(1)}, u32[]{:S(2)}, u32[]{:S(2)}) %collective-permute-start.15) | collective-permute-done | bytes 196640 | tf_op jit(solution)/shard_map/ppermute | solution.py:28
  29.9 2.3 %collective-permute-done.16.refs_0_ = bf16[12,32,256]{2,1,0:T(8,128)(2,1)S(1)} collective-permute-done((bf16[12,32,256]{2,1,0:T(8,128)(2,1)S(1)}, bf16[12,32,256]{2,1,0:T(8,128)(2,1)S(1)}, u32[]{:S(2)}, u32[]{:S(2)}) %collective-permute-start.16) | collective-permute-done | bytes 196640 | tf_op jit(solution)/shard_map/ppermute | solution.py:28
  32.3 1.8 %collective-permute-done.17.refs_1_ = bf16[12,32,256]{2,1,0:T(8,128)(2,1)S(1)} collective-permute-done((bf16[12,32,256]{2,1,0:T(8,128)(2,1)S(1)}, bf16[12,32,256]{2,1,0:T(8,128)(2,1)S(1)}, u32[]{:S(2)}, u32[]{:S(2)}) %collective-permute-start.17) | collective-permute-done | bytes 196640 | tf_op jit(solution)/shard_map/ppermute | solution.py:28
  37.8 1.8 %collective-permute-start.20 = (bf16[5,32,256]{2,1,0:T(8,128)(2,1)S(1)}, bf16[5,32,256]{2,1,0:T(8,128)(2,1)S(1)}, u32[]{:S(2)}, u32[]{:S(2)}) collective-permute-start(bf16[5,32,256]{2,1,0:T(8,128)(2,1)S(1)} %get-tuple-element.67), channel_id=1, source_target_pairs={{0,12},{1,13},{2,14},{3,15},{4,8},{5,9},{6,10},{7,11},{8,20},{9,21... | collective-permute-start | bytes 245768 | tf_op jit(solution)/shard_map/ppermute | solution.py:28
  41.0 2.5 %collective-permute-start.21 = (bf16[5,32,256]{2,1,0:T(8,128)(2,1)S(1)}, bf16[5,32,256]{2,1,0:T(8,128)(2,1)S(1)}, u32[]{:S(2)}, u32[]{:S(2)}) collective-permute-start(bf16[5,32,256]{2,1,0:T(8,128)(2,1)S(1)} %get-tuple-element.68), channel_id=1, source_target_pairs={{0,14},{1,15},{2,12},{3,13},{4,10},{5,11},{6,8},{7,9},{8,22},{9,23... | collective-permute-start | bytes 245768 | tf_op jit(solution)/shard_map/ppermute | solution.py:28
  43.5 3.3 %collective-permute-start.18 = (bf16[5,32,256]{2,1,0:T(8,128)(2,1)S(1)}, bf16[5,32,256]{2,1,0:T(8,128)(2,1)S(1)}, u32[]{:S(2)}, u32[]{:S(2)}) collective-permute-start(bf16[5,32,256]{2,1,0:T(8,128)(2,1)S(1)} %get-tuple-element.62.after_ref.refs_13_), channel_id=1, source_target_pairs={{0,8},{1,9},{2,10},{3,11},{4,12},{5,13},{6,14},{7,15},{8,16},{9,17... | collective-permute-start | bytes 245768 | tf_op jit(solution)/shard_map/ppermute | solution.py:28
  47.4 1.7 %collective-permute-done.21.refs_8_ = bf16[5,32,256]{2,1,0:T(8,128)(2,1)S(1)} collective-permute-done((bf16[5,32,256]{2,1,0:T(8,128)(2,1)S(1)}, bf16[5,32,256]{2,1,0:T(8,128)(2,1)S(1)}, u32[]{:S(2)}, u32[]{:S(2)}) %collective-permute-start.21) | collective-permute-done | bytes 81952 | tf_op jit(solution)/shard_map/ppermute | solution.py:28
  53.1 2.1 %collective-permute-start.33 = (bf16[12,32,256]{2,1,0:T(8,128)(2,1)S(1)}, bf16[12,32,256]{2,1,0:T(8,128)(2,1)S(1)}, u32[]{:S(2)}, u32[]{:S(2)}) collective-permute-start(bf16[12,32,256]{2,1,0:T(8,128)(2,1)S(1)} %get-tuple-element.70), channel_id=1, source_target_pairs={{0,2},{1,3},{2,0},{3,1},{4,6},{5,7},{6,4},{7,5},{8,10},{9,11},{10,... | collective-permute-start | bytes 589832 | tf_op jit(solution)/shard_map/ppermute | solution.py:28
  56.8 1.9 %shard_map.60 = (bf16[640,256]{1,0:T(8,128)(2,1)S(1)}, bf16[640,640]{1,0:T(8,128)(2,1)S(1)}, bf16[640,1536]{1,0:T(8,128)(2,1)S(1)}) custom-call(bf16[5,32,256]{2,1,0:T(8,128)(2,1)S(1)} %get-tuple-element.62.after_ref.refs_13_, bf16[4,640,256]{2,1,0:T(8,128)(2,1)} %rhs_hbm.7, bf16[4,640,640]{2,1,0:T(8,128)(2,1)} %inv_hbm.7, bf16[3,12,4,32,640]{4,3,2,1,0:T(8,128)(2,1)} %bitcast.9), custom_call_target="tpu_custom_call" | custom-call | bytes 3112960 | tf_op jit(solution)/shard_map/pallas_call | solution.py:274
  58.7 2.3 %collective-permute-done.33.refs_1_ = bf16[12,32,256]{2,1,0:T(8,128)(2,1)S(1)} collective-permute-done((bf16[12,32,256]{2,1,0:T(8,128)(2,1)S(1)}, bf16[12,32,256]{2,1,0:T(8,128)(2,1)S(1)}, u32[]{:S(2)}, u32[]{:S(2)}) %collective-permute-start.33) | collective-permute-done | bytes 196640 | tf_op jit(solution)/shard_map/ppermute | solution.py:28
  61.6 4.6 %collective-permute-done.34.refs_0_ = bf16[12,32,256]{2,1,0:T(8,128)(2,1)S(1)} collective-permute-done((bf16[12,32,256]{2,1,0:T(8,128)(2,1)S(1)}, bf16[12,32,256]{2,1,0:T(8,128)(2,1)S(1)}, u32[]{:S(2)}, u32[]{:S(2)}) %collective-permute-start.34) | collective-permute-done | bytes 196640 | tf_op jit(solution)/shard_map/ppermute | solution.py:28
  69.1 1.9 %collective-permute-start.38 = (bf16[5,32,256]{2,1,0:T(8,128)(2,1)S(1)}, bf16[5,32,256]{2,1,0:T(8,128)(2,1)S(1)}, u32[]{:S(2)}, u32[]{:S(2)}) collective-permute-start(bf16[5,32,256]{2,1,0:T(8,128)(2,1)S(1)} %get-tuple-element.79), channel_id=1, source_target_pairs={{0,12},{1,13},{2,14},{3,15},{4,8},{5,9},{6,10},{7,11},{8,20},{9,21... | collective-permute-start | bytes 245768 | tf_op jit(solution)/shard_map/ppermute | solution.py:28
  72.2 3.6 %collective-permute-start.39 = (bf16[5,32,256]{2,1,0:T(8,128)(2,1)S(1)}, bf16[5,32,256]{2,1,0:T(8,128)(2,1)S(1)}, u32[]{:S(2)}, u32[]{:S(2)}) collective-permute-start(bf16[5,32,256]{2,1,0:T(8,128)(2,1)S(1)} %get-tuple-element.80), channel_id=1, source_target_pairs={{0,14},{1,15},{2,12},{3,13},{4,10},{5,11},{6,8},{7,9},{8,22},{9,23... | collective-permute-start | bytes 245768 | tf_op jit(solution)/shard_map/ppermute | solution.py:28
  75.8 1.9 %collective-permute-start.36 = (bf16[5,32,256]{2,1,0:T(8,128)(2,1)S(1)}, bf16[5,32,256]{2,1,0:T(8,128)(2,1)S(1)}, u32[]{:S(2)}, u32[]{:S(2)}) collective-permute-start(bf16[5,32,256]{2,1,0:T(8,128)(2,1)S(1)} %get-tuple-element.74.after_ref.refs_13_), channel_id=1, source_target_pairs={{0,8},{1,9},{2,10},{3,11},{4,12},{5,13},{6,14},{7,15},{8,16},{9,17... | collective-permute-start | bytes 245768 | tf_op jit(solution)/shard_map/ppermute | solution.py:28
  78.3 2.0 %collective-permute-done.39.refs_8_ = bf16[5,32,256]{2,1,0:T(8,128)(2,1)S(1)} collective-permute-done((bf16[5,32,256]{2,1,0:T(8,128)(2,1)S(1)}, bf16[5,32,256]{2,1,0:T(8,128)(2,1)S(1)}, u32[]{:S(2)}, u32[]{:S(2)}) %collective-permute-start.39) | collective-permute-done | bytes 81952 | tf_op jit(solution)/shard_map/ppermute | solution.py:28
  80.8 3.1 %collective-permute-done.36.refs_5_ = bf16[5,32,256]{2,1,0:T(8,128)(2,1)S(1)} collective-permute-done((bf16[5,32,256]{2,1,0:T(8,128)(2,1)S(1)}, bf16[5,32,256]{2,1,0:T(8,128)(2,1)S(1)}, u32[]{:S(2)}, u32[]{:S(2)}) %collective-permute-start.36) | collective-permute-done | bytes 81952 | tf_op jit(solution)/shard_map/ppermute | solution.py:28
  91.2 1.9 %shard_map.64 = (bf16[640,256]{1,0:T(8,128)(2,1)S(1)}, bf16[640,640]{1,0:T(8,128)(2,1)S(1)}, bf16[640,1536]{1,0:T(8,128)(2,1)S(1)}) custom-call(bf16[5,32,256]{2,1,0:T(8,128)(2,1)S(1)} %get-tuple-element.74.after_ref.refs_13_, bf16[4,640,256]{2,1,0:T(8,128)(2,1)} %rhs_hbm.7, bf16[4,640,640]{2,1,0:T(8,128)(2,1)} %inv_hbm.7, bf16[3,12,4,32,640]{4,3,2,1,0:T(8,128)(2,1)} %bitcast.10), custom_call_target="tpu_custom_call" | custom-call | bytes 3112960 | tf_op jit(solution)/shard_map/pallas_call | solution.py:274
  94.5 3.3 %collective-permute-done.52.refs_0_ = bf16[12,32,256]{2,1,0:T(8,128)(2,1)S(1)} collective-permute-done((bf16[12,32,256]{2,1,0:T(8,128)(2,1)S(1)}, bf16[12,32,256]{2,1,0:T(8,128)(2,1)S(1)}, u32[]{:S(2)}, u32[]{:S(2)}) %collective-permute-start.52) | collective-permute-done | bytes 196640 | tf_op jit(solution)/shard_map/ppermute | solution.py:28
  97.8 1.8 %shard_map.70 = f32[4,640,256]{2,1,0:T(8,128)} custom-call(s32[1,3]{1,0:T(1,128)S(1)} %bitcast.7, f32[640,256]{1,0:T(8,128)S(1)} %shard_map.66.base_ref, bf16[640,640]{1,0:T(8,128)(2,1)S(1)} %get-tuple-element.83.inv_ref, bf16[640,1536]{1,0:T(8,128)(2,1)S(1)} %get-tuple-element.76.turned_ref, ...), custom_call_target="tpu_custom_call", output_to_operand_aliasing={{}: (6, {})} | custom-call | flops 356515840 | bytes 3997696 | tf_op jit(solution)/shard_map/pallas_call | solution.py:339
  (102 shorter events, 40.4 us)
Async XLA Ops:
  1.6 9.8 %collective-permute-start.4 = (bf16[5,32,256]{2,1,0:T(8,128)(2,1)S(1)}, bf16[5,32,256]{2,1,0:T(8,128)(2,1)S(1)}, u32[]{:S(2)}, u32[]{:S(2)}) collective-permute-start(bf16[5,32,256]{2,1,0:T(8,128)(2,1)S(1)} %get-tuple-element.54), channel_id=1, source_target_pairs={{0,10},{1,11},{2,8},{3,9},{4,14},{5,15},{6,12},{7,13},{8,18},{9,19... | collective-permute-start | bytes 245768 | tf_op jit(solution)/shard_map/ppermute | solution.py:28
  5.7 7.7 %collective-permute-start.5 = (bf16[5,32,256]{2,1,0:T(8,128)(2,1)S(1)}, bf16[5,32,256]{2,1,0:T(8,128)(2,1)S(1)}, u32[]{:S(2)}, u32[]{:S(2)}) collective-permute-start(bf16[5,32,256]{2,1,0:T(8,128)(2,1)S(1)} %get-tuple-element.55), channel_id=1, source_target_pairs={{0,12},{1,13},{2,14},{3,15},{4,8},{5,9},{6,10},{7,11},{8,20},{9,21... | collective-permute-start | bytes 245768 | tf_op jit(solution)/shard_map/ppermute | solution.py:28
  8.2 8.9 %collective-permute-start.6 = (bf16[5,32,256]{2,1,0:T(8,128)(2,1)S(1)}, bf16[5,32,256]{2,1,0:T(8,128)(2,1)S(1)}, u32[]{:S(2)}, u32[]{:S(2)}) collective-permute-start(bf16[5,32,256]{2,1,0:T(8,128)(2,1)S(1)} %get-tuple-element.56), channel_id=1, source_target_pairs={{0,14},{1,15},{2,12},{3,13},{4,10},{5,11},{6,8},{7,9},{8,22},{9,23... | collective-permute-start | bytes 245768 | tf_op jit(solution)/shard_map/ppermute | solution.py:28
  9.7 8.0 %collective-permute-start = (bf16[6,32,256]{2,1,0:T(8,128)(2,1)S(1)}, bf16[6,32,256]{2,1,0:T(8,128)(2,1)S(1)}, u32[]{:S(2)}, u32[]{:S(2)}) collective-permute-start(bf16[6,32,256]{2,1,0:T(8,128)(2,1)S(1)} %get-tuple-element.51), channel_id=1, source_target_pairs={{0,2},{1,3},{2,0},{3,1},{4,6},{5,7},{6,4},{7,5},{8,10},{9,11},{10,... | collective-permute-start | bytes 294920 | tf_op jit(solution)/shard_map/ppermute | solution.py:28
  11.4 7.6 %collective-permute-start.1 = (bf16[6,32,256]{2,1,0:T(8,128)(2,1)S(1)}, bf16[6,32,256]{2,1,0:T(8,128)(2,1)S(1)}, u32[]{:S(2)}, u32[]{:S(2)}) collective-permute-start(bf16[6,32,256]{2,1,0:T(8,128)(2,1)S(1)} %get-tuple-element.52), channel_id=1, source_target_pairs={{0,4},{1,5},{2,6},{3,7},{4,0},{5,1},{6,2},{7,3},{8,12},{9,13},{10,... | collective-permute-start | bytes 294920 | tf_op jit(solution)/shard_map/ppermute | solution.py:28
  21.6 7.8 %collective-permute-start.15 = (bf16[12,32,256]{2,1,0:T(8,128)(2,1)S(1)}, bf16[12,32,256]{2,1,0:T(8,128)(2,1)S(1)}, u32[]{:S(2)}, u32[]{:S(2)}) collective-permute-start(bf16[12,32,256]{2,1,0:T(8,128)(2,1)S(1)} %get-tuple-element.58), channel_id=1, source_target_pairs={{0,2},{1,3},{2,0},{3,1},{4,6},{5,7},{6,4},{7,5},{8,10},{9,11},{10,... | collective-permute-start | bytes 589832 | tf_op jit(solution)/shard_map/ppermute | solution.py:28
  22.0 10.3 %collective-permute-start.16 = (bf16[12,32,256]{2,1,0:T(8,128)(2,1)S(1)}, bf16[12,32,256]{2,1,0:T(8,128)(2,1)S(1)}, u32[]{:S(2)}, u32[]{:S(2)}) collective-permute-start(bf16[12,32,256]{2,1,0:T(8,128)(2,1)S(1)} %get-tuple-element.60), channel_id=1, source_target_pairs={{0,4},{1,5},{2,6},{3,7},{4,0},{5,1},{6,2},{7,3},{8,12},{9,13},{10,... | collective-permute-start | bytes 589832 | tf_op jit(solution)/shard_map/ppermute | solution.py:28
  23.4 10.6 %collective-permute-start.17 = (bf16[12,32,256]{2,1,0:T(8,128)(2,1)S(1)}, bf16[12,32,256]{2,1,0:T(8,128)(2,1)S(1)}, u32[]{:S(2)}, u32[]{:S(2)}) collective-permute-start(bf16[12,32,256]{2,1,0:T(8,128)(2,1)S(1)} %get-tuple-element.61), channel_id=1, source_target_pairs={{0,6},{1,7},{2,4},{3,5},{4,2},{5,3},{6,0},{7,1},{8,14},{9,15},{10,... | collective-permute-start | bytes 589832 | tf_op jit(solution)/shard_map/ppermute | solution.py:28
  35.8 7.7 %collective-permute-start.19 = (bf16[5,32,256]{2,1,0:T(8,128)(2,1)S(1)}, bf16[5,32,256]{2,1,0:T(8,128)(2,1)S(1)}, u32[]{:S(2)}, u32[]{:S(2)}) collective-permute-start(bf16[5,32,256]{2,1,0:T(8,128)(2,1)S(1)} %get-tuple-element.66), channel_id=1, source_target_pairs={{0,10},{1,11},{2,8},{3,9},{4,14},{5,15},{6,12},{7,13},{8,18},{9,19... | collective-permute-start | bytes 245768 | tf_op jit(solution)/shard_map/ppermute | solution.py:28
  37.8 9.1 %collective-permute-start.20 = (bf16[5,32,256]{2,1,0:T(8,128)(2,1)S(1)}, bf16[5,32,256]{2,1,0:T(8,128)(2,1)S(1)}, u32[]{:S(2)}, u32[]{:S(2)}) collective-permute-start(bf16[5,32,256]{2,1,0:T(8,128)(2,1)S(1)} %get-tuple-element.67), channel_id=1, source_target_pairs={{0,12},{1,13},{2,14},{3,15},{4,8},{5,9},{6,10},{7,11},{8,20},{9,21... | collective-permute-start | bytes 245768 | tf_op jit(solution)/shard_map/ppermute | solution.py:28
  39.6 7.3 %collective-permute-start.28 = (bf16[5,32,256]{2,1,0:T(8,128)(2,1)S(1)}, bf16[5,32,256]{2,1,0:T(8,128)(2,1)S(1)}, u32[]{:S(2)}, u32[]{:S(2)}) collective-permute-start(bf16[5,32,256]{2,1,0:T(8,128)(2,1)S(1)} %get-tuple-element.68), channel_id=1, source_target_pairs={{0,6},{1,7},{2,4},{3,5},{4,2},{5,3},{6,0},{7,1},{8,14},{9,15},{10,... | collective-permute-start | bytes 245768 | tf_op jit(solution)/shard_map/ppermute | solution.py:28
  41.0 8.0 %collective-permute-start.21 = (bf16[5,32,256]{2,1,0:T(8,128)(2,1)S(1)}, bf16[5,32,256]{2,1,0:T(8,128)(2,1)S(1)}, u32[]{:S(2)}, u32[]{:S(2)}) collective-permute-start(bf16[5,32,256]{2,1,0:T(8,128)(2,1)S(1)} %get-tuple-element.68), channel_id=1, source_target_pairs={{0,14},{1,15},{2,12},{3,13},{4,10},{5,11},{6,8},{7,9},{8,22},{9,23... | collective-permute-start | bytes 245768 | tf_op jit(solution)/shard_map/ppermute | solution.py:28
  43.5 7.6 %collective-permute-start.18 = (bf16[5,32,256]{2,1,0:T(8,128)(2,1)S(1)}, bf16[5,32,256]{2,1,0:T(8,128)(2,1)S(1)}, u32[]{:S(2)}, u32[]{:S(2)}) collective-permute-start(bf16[5,32,256]{2,1,0:T(8,128)(2,1)S(1)} %get-tuple-element.62.after_ref.refs_13_), channel_id=1, source_target_pairs={{0,8},{1,9},{2,10},{3,11},{4,12},{5,13},{6,14},{7,15},{8,16},{9,17... | collective-permute-start | bytes 245768 | tf_op jit(solution)/shard_map/ppermute | solution.py:28
  53.1 7.9 %collective-permute-start.33 = (bf16[12,32,256]{2,1,0:T(8,128)(2,1)S(1)}, bf16[12,32,256]{2,1,0:T(8,128)(2,1)S(1)}, u32[]{:S(2)}, u32[]{:S(2)}) collective-permute-start(bf16[12,32,256]{2,1,0:T(8,128)(2,1)S(1)} %get-tuple-element.70), channel_id=1, source_target_pairs={{0,2},{1,3},{2,0},{3,1},{4,6},{5,7},{6,4},{7,5},{8,10},{9,11},{10,... | collective-permute-start | bytes 589832 | tf_op jit(solution)/shard_map/ppermute | solution.py:28
  55.3 10.9 %collective-permute-start.34 = (bf16[12,32,256]{2,1,0:T(8,128)(2,1)S(1)}, bf16[12,32,256]{2,1,0:T(8,128)(2,1)S(1)}, u32[]{:S(2)}, u32[]{:S(2)}) collective-permute-start(bf16[12,32,256]{2,1,0:T(8,128)(2,1)S(1)} %get-tuple-element.72), channel_id=1, source_target_pairs={{0,4},{1,5},{2,6},{3,7},{4,0},{5,1},{6,2},{7,3},{8,12},{9,13},{10,... | collective-permute-start | bytes 589832 | tf_op jit(solution)/shard_map/ppermute | solution.py:28
  56.1 10.0 %collective-permute-start.35 = (bf16[12,32,256]{2,1,0:T(8,128)(2,1)S(1)}, bf16[12,32,256]{2,1,0:T(8,128)(2,1)S(1)}, u32[]{:S(2)}, u32[]{:S(2)}) collective-permute-start(bf16[12,32,256]{2,1,0:T(8,128)(2,1)S(1)} %get-tuple-element.73), channel_id=1, source_target_pairs={{0,6},{1,7},{2,4},{3,5},{4,2},{5,3},{6,0},{7,1},{8,14},{9,15},{10,... | collective-permute-start | bytes 589832 | tf_op jit(solution)/shard_map/ppermute | solution.py:28
  67.9 7.9 %collective-permute-start.37 = (bf16[5,32,256]{2,1,0:T(8,128)(2,1)S(1)}, bf16[5,32,256]{2,1,0:T(8,128)(2,1)S(1)}, u32[]{:S(2)}, u32[]{:S(2)}) collective-permute-start(bf16[5,32,256]{2,1,0:T(8,128)(2,1)S(1)} %get-tuple-element.78), channel_id=1, source_target_pairs={{0,10},{1,11},{2,8},{3,9},{4,14},{5,15},{6,12},{7,13},{8,18},{9,19... | collective-permute-start | bytes 245768 | tf_op jit(solution)/shard_map/ppermute | solution.py:28
  67.9 7.9 %collective-permute-start.45 = (bf16[5,32,256]{2,1,0:T(8,128)(2,1)S(1)}, bf16[5,32,256]{2,1,0:T(8,128)(2,1)S(1)}, u32[]{:S(2)}, u32[]{:S(2)}) collective-permute-start(bf16[5,32,256]{2,1,0:T(8,128)(2,1)S(1)} %get-tuple-element.79), channel_id=1, source_target_pairs={{0,4},{1,5},{2,6},{3,7},{4,0},{5,1},{6,2},{7,3},{8,12},{9,13},{10,... | collective-permute-start | bytes 245768 | tf_op jit(solution)/shard_map/ppermute | solution.py:28
  69.1 8.7 %collective-permute-start.38 = (bf16[5,32,256]{2,1,0:T(8,128)(2,1)S(1)}, bf16[5,32,256]{2,1,0:T(8,128)(2,1)S(1)}, u32[]{:S(2)}, u32[]{:S(2)}) collective-permute-start(bf16[5,32,256]{2,1,0:T(8,128)(2,1)S(1)} %get-tuple-element.79), channel_id=1, source_target_pairs={{0,12},{1,13},{2,14},{3,15},{4,8},{5,9},{6,10},{7,11},{8,20},{9,21... | collective-permute-start | bytes 245768 | tf_op jit(solution)/shard_map/ppermute | solution.py:28
  72.2 8.0 %collective-permute-start.39 = (bf16[5,32,256]{2,1,0:T(8,128)(2,1)S(1)}, bf16[5,32,256]{2,1,0:T(8,128)(2,1)S(1)}, u32[]{:S(2)}, u32[]{:S(2)}) collective-permute-start(bf16[5,32,256]{2,1,0:T(8,128)(2,1)S(1)} %get-tuple-element.80), channel_id=1, source_target_pairs={{0,14},{1,15},{2,12},{3,13},{4,10},{5,11},{6,8},{7,9},{8,22},{9,23... | collective-permute-start | bytes 245768 | tf_op jit(solution)/shard_map/ppermute | solution.py:28
  75.8 8.1 %collective-permute-start.36 = (bf16[5,32,256]{2,1,0:T(8,128)(2,1)S(1)}, bf16[5,32,256]{2,1,0:T(8,128)(2,1)S(1)}, u32[]{:S(2)}, u32[]{:S(2)}) collective-permute-start(bf16[5,32,256]{2,1,0:T(8,128)(2,1)S(1)} %get-tuple-element.74.after_ref.refs_13_), channel_id=1, source_target_pairs={{0,8},{1,9},{2,10},{3,11},{4,12},{5,13},{6,14},{7,15},{8,16},{9,17... | collective-permute-start | bytes 245768 | tf_op jit(solution)/shard_map/ppermute | solution.py:28
  85.9 8.0 %collective-permute-start.51 = (bf16[12,32,256]{2,1,0:T(8,128)(2,1)S(1)}, bf16[12,32,256]{2,1,0:T(8,128)(2,1)S(1)}, u32[]{:S(2)}, u32[]{:S(2)}) collective-permute-start(bf16[12,32,256]{2,1,0:T(8,128)(2,1)S(1)} %get-tuple-element.82), channel_id=1, source_target_pairs={{0,2},{1,3},{2,0},{3,1},{4,6},{5,7},{6,4},{7,5},{8,10},{9,11},{10,... | collective-permute-start | bytes 589832 | tf_op jit(solution)/shard_map/ppermute | solution.py:28
  86.9 10.9 %collective-permute-start.52 = (bf16[12,32,256]{2,1,0:T(8,128)(2,1)S(1)}, bf16[12,32,256]{2,1,0:T(8,128)(2,1)S(1)}, u32[]{:S(2)}, u32[]{:S(2)}) collective-permute-start(bf16[12,32,256]{2,1,0:T(8,128)(2,1)S(1)} %get-tuple-element.84), channel_id=1, source_target_pairs={{0,4},{1,5},{2,6},{3,7},{4,0},{5,1},{6,2},{7,3},{8,12},{9,13},{10,... | collective-permute-start | bytes 589832 | tf_op jit(solution)/shard_map/ppermute | solution.py:28
  87.8 9.9 %collective-permute-start.53 = (bf16[12,32,256]{2,1,0:T(8,128)(2,1)S(1)}, bf16[12,32,256]{2,1,0:T(8,128)(2,1)S(1)}, u32[]{:S(2)}, u32[]{:S(2)}) collective-permute-start(bf16[12,32,256]{2,1,0:T(8,128)(2,1)S(1)} %get-tuple-element.85), channel_id=1, source_target_pairs={{0,6},{1,7},{2,4},{3,5},{4,2},{5,3},{6,0},{7,1},{8,14},{9,15},{10,... | collective-permute-start | bytes 589832 | tf_op jit(solution)/shard_map/ppermute | solution.py:28
  (31 other events, 110.3 us)

commit v2 on v1

--- a/solution.py
+++ b/solution.py
@@ -57,11 +57,13 @@
         copy.wait()
 
 
-def solve_rows(inv_ref, reduced_ref, x_ref, piece_refs, tile, row_done=None):
+def solve_rows(inv_ref, reduced_ref, x_ref, piece_refs, tile, row_start=None, row_done=None):
     width = inv_ref.shape[0]
     quarter = tile // CHIPS
     per_node = width // tile
     for i in reversed(range(per_node)):
+        if row_start is not None:
+            row_start(i)
         x_ref[i * tile : (i + 1) * tile, :] = jnp.dot(
             inv_ref[i * tile : (i + 1) * tile, i * tile :],
             reduced_ref[i * tile :, :],
@@ -96,24 +98,39 @@
 def first_kernel(tile, list_hbm, rhs_hbm, inv_hbm, x_ref, *refs):
     piece_refs, noted_refs = refs[:CHIPS], refs[CHIPS:-5]
     rhs_ref, inv_ref, list_ref, note_ref, sems = refs[-5:]
-    run_copies(
-        [
-            pltpu.make_async_copy(rhs_hbm.at[0], rhs_ref, sems.at[0]),
-            pltpu.make_async_copy(inv_hbm.at[0], inv_ref, sems.at[1]),
-            pltpu.make_async_copy(list_hbm, list_ref, sems.at[2]),
-        ]
-    )
     levels, _, slots = list_ref.shape
-    per_node = inv_ref.shape[0] // tile
+    width = inv_ref.shape[0]
+    per_node = width // tile
     pool = 2 * GROUP * per_node
-    solve_rows(inv_ref, rhs_ref, x_ref, piece_refs, tile)
+    split = (per_node + 1) // 2 * tile
+    halves = [
+        pltpu.make_async_copy(inv_hbm.at[0, pl.ds(first, size)], inv_ref.at[pl.ds(first, size)], sem)
+        for first, size, sem in (
+            (split, width - split, sems.at[0]),
+            (0, split, sems.at[1]),
+        )
+    ]
+    list_copy = pltpu.make_async_copy(list_hbm, list_ref, sems.at[2])
+    rhs_copy = pltpu.make_async_copy(rhs_hbm.at[0], rhs_ref, sems.at[3])
+    for copy in (list_copy, rhs_copy, *halves):
+        copy.start()
+    list_copy.wait()
     note_ref[...] = jnp.zeros_like(note_ref)
     for relative in range(CHIPS):
         for level in range(levels):
             places = places_of(list_ref[level], relative, levels, pool, per_node)
             note_ref[level : level + 1, :slots] = places.astype(jnp.float32)
+        noted_refs[relative][per_node] = note_ref[...].astype(jnp.bfloat16)
+    rhs_copy.wait()
+    halves[0].wait()
+
+    def row_start(i):
+        if i == split // tile - 1:
+            halves[1].wait()
+
+    solve_rows(inv_ref, rhs_ref, x_ref, piece_refs, tile, row_start=row_start)
+    for relative in range(CHIPS):
         noted_refs[relative][:per_node] = piece_refs[relative][...]
-        noted_refs[relative][per_node] = note_ref[...].astype(jnp.bfloat16)
 
 
 def load_kernel(level, after_ref, rhs_hbm, inv_hbm, factor_hbm, rhs_ref, inv_ref, turned_ref, *scratch):
@@ -194,7 +211,7 @@
         rows = pl.ds(i * tile, tile)
         return pltpu.make_async_copy(x_ref.at[rows], out_hbm.at[level, rows], sems.at[i])
 
-    solve_rows(inv_ref, reduced_ref, x_ref, (), tile, lambda i: row_copy(i).start())
+    solve_rows(inv_ref, reduced_ref, x_ref, (), tile, row_done=lambda i: row_copy(i).start())
     for i in range(inv_ref.shape[0] // tile):
         row_copy(i).wait()
 
@@ -256,7 +273,7 @@
             pltpu.VMEM((width, width), half),
             pltpu.VMEM(tile_list.shape, jnp.int32),
             pltpu.VMEM((quarter, columns), jnp.float32),
-            semaphores((3,)),
+            semaphores((4,)),
         ],
     )(tile_list, rhs, inv_diag)
     pieces, noted = outputs[:CHIPS], outputs[CHIPS:]

time: 99.8 us -> 99.8 us (level)
  no operation moved by 1% of the time
where the time goes in v2:
time: 99.8 us; the launch traced here: 99.5 us
  starting transfers between devices  50.1 us (50%)
  waiting for transfers between devices  33.2 us (33%)
  Pallas kernels  16 us (16%)
    ppermute x30, starting transfers between devices, send(): return lax.ppermute(value, 'nodes', route)  45.3 us
    ppermute x30, waiting for transfers between devices, send(): return lax.ppermute(value, 'nodes', route)  29.6 us
    pallas_call x3, Pallas kernels, body(): call(functools.partial(load_kernel, level), (jax.ShapeDtypeStruct((width,...  5.7 us
    ppermute x24, starting transfers between devices, swap(): return lax.ppermute(value, 'nodes', [(i, i ^ 1) for i in range(size)])  4.81 us
    ppermute x24, waiting for transfers between devices, swap(): return lax.ppermute(value, 'nodes', [(i, i ^ 1) for i in range(size)])  3.65 us
    pallas_call x3, Pallas kernels, body(): call(functools.partial(store_kernel, level - 1), out_shape, [VMEM] if lev...  2.54 us
    pallas_call x2, Pallas kernels, body(): level_call(out_shape=shapes, in_specs=in_specs, out_specs=[VMEM] * len(sh...  2.19 us
  transfers between devices with their start and end apart: 54, of which 23 were waited for; matrix products, arithmetic and copies ran while one was open for 0% of the time, Pallas kernels for 10%

profile of v2, /device:TPU:0, one launch (start us, length us, event | category | flops | bytes accessed | tf_op | source)
XLA Modules:
  0.0 99.5 jit_solution(3955663799648286744)
XLA Ops:
  1.6 4.0 %collective-permute-start.4 = (bf16[5,32,256]{2,1,0:T(8,128)(2,1)S(1)}, bf16[5,32,256]{2,1,0:T(8,128)(2,1)S(1)}, u32[]{:S(2)}, u32[]{:S(2)}) collective-permute-start(bf16[5,32,256]{2,1,0:T(8,128)(2,1)S(1)} %get-tuple-element.54), channel_id=1, source_target_pairs={{0,10},{1,11},{2,8},{3,9},{4,14},{5,15},{6,12},{7,13},{8,18},{9,19... | collective-permute-start | bytes 245768 | tf_op jit(solution)/shard_map/ppermute | solution.py:28
  5.7 2.5 %collective-permute-start.5 = (bf16[5,32,256]{2,1,0:T(8,128)(2,1)S(1)}, bf16[5,32,256]{2,1,0:T(8,128)(2,1)S(1)}, u32[]{:S(2)}, u32[]{:S(2)}) collective-permute-start(bf16[5,32,256]{2,1,0:T(8,128)(2,1)S(1)} %get-tuple-element.55), channel_id=1, source_target_pairs={{0,12},{1,13},{2,14},{3,15},{4,8},{5,9},{6,10},{7,11},{8,20},{9,21... | collective-permute-start | bytes 245768 | tf_op jit(solution)/shard_map/ppermute | solution.py:28
  14.6 2.6 %collective-permute-done.6.refs_7_ = bf16[5,32,256]{2,1,0:T(8,128)(2,1)S(1)} collective-permute-done((bf16[5,32,256]{2,1,0:T(8,128)(2,1)S(1)}, bf16[5,32,256]{2,1,0:T(8,128)(2,1)S(1)}, u32[]{:S(2)}, u32[]{:S(2)}) %collective-permute-start.6) | collective-permute-done | bytes 81952 | tf_op jit(solution)/shard_map/ppermute | solution.py:28
  23.4 1.7 %collective-permute-start.17 = (bf16[12,32,256]{2,1,0:T(8,128)(2,1)S(1)}, bf16[12,32,256]{2,1,0:T(8,128)(2,1)S(1)}, u32[]{:S(2)}, u32[]{:S(2)}) collective-permute-start(bf16[12,32,256]{2,1,0:T(8,128)(2,1)S(1)} %get-tuple-element.61), channel_id=1, source_target_pairs={{0,6},{1,7},{2,4},{3,5},{4,2},{5,3},{6,0},{7,1},{8,14},{9,15},{10,... | collective-permute-start | bytes 589832 | tf_op jit(solution)/shard_map/ppermute | solution.py:28
  25.1 1.9 %shard_map.56 = (bf16[640,256]{1,0:T(8,128)(2,1)S(1)}, bf16[640,640]{1,0:T(8,128)(2,1)S(1)}, bf16[640,1536]{1,0:T(8,128)(2,1)S(1)}) custom-call(bf16[5,32,256]{2,1,0:T(8,128)(2,1)S(1)} %get-tuple-element.47.after_ref, bf16[4,640,256]{2,1,0:T(8,128)(2,1)} %rhs_hbm.7, bf16[4,640,640]{2,1,0:T(8,128)(2,1)} %inv_hbm.7, bf16[3,12,4,32,640]{4,3,2,1,0:T(8,128)(2,1)} %bitcast.8), custom_call_target="tpu_custom_call" | custom-call | bytes 3112960 | tf_op jit(solution)/shard_map/pallas_call | solution.py:291
  27.0 2.4 %collective-permute-done.15.refs_1_ = bf16[12,32,256]{2,1,0:T(8,128)(2,1)S(1)} collective-permute-done((bf16[12,32,256]{2,1,0:T(8,128)(2,1)S(1)}, bf16[12,32,256]{2,1,0:T(8,128)(2,1)S(1)}, u32[]{:S(2)}, u32[]{:S(2)}) %collective-permute-start.15) | collective-permute-done | bytes 196640 | tf_op jit(solution)/shard_map/ppermute | solution.py:28
  29.9 2.3 %collective-permute-done.16.refs_0_ = bf16[12,32,256]{2,1,0:T(8,128)(2,1)S(1)} collective-permute-done((bf16[12,32,256]{2,1,0:T(8,128)(2,1)S(1)}, bf16[12,32,256]{2,1,0:T(8,128)(2,1)S(1)}, u32[]{:S(2)}, u32[]{:S(2)}) %collective-permute-start.16) | collective-permute-done | bytes 196640 | tf_op jit(solution)/shard_map/ppermute | solution.py:28
  32.3 1.8 %collective-permute-done.17.refs_1_ = bf16[12,32,256]{2,1,0:T(8,128)(2,1)S(1)} collective-permute-done((bf16[12,32,256]{2,1,0:T(8,128)(2,1)S(1)}, bf16[12,32,256]{2,1,0:T(8,128)(2,1)S(1)}, u32[]{:S(2)}, u32[]{:S(2)}) %collective-permute-start.17) | collective-permute-done | bytes 196640 | tf_op jit(solution)/shard_map/ppermute | solution.py:28
  37.8 1.8 %collective-permute-start.20 = (bf16[5,32,256]{2,1,0:T(8,128)(2,1)S(1)}, bf16[5,32,256]{2,1,0:T(8,128)(2,1)S(1)}, u32[]{:S(2)}, u32[]{:S(2)}) collective-permute-start(bf16[5,32,256]{2,1,0:T(8,128)(2,1)S(1)} %get-tuple-element.67), channel_id=1, source_target_pairs={{0,12},{1,13},{2,14},{3,15},{4,8},{5,9},{6,10},{7,11},{8,20},{9,21... | collective-permute-start | bytes 245768 | tf_op jit(solution)/shard_map/ppermute | solution.py:28
  41.0 2.5 %collective-permute-start.21 = (bf16[5,32,256]{2,1,0:T(8,128)(2,1)S(1)}, bf16[5,32,256]{2,1,0:T(8,128)(2,1)S(1)}, u32[]{:S(2)}, u32[]{:S(2)}) collective-permute-start(bf16[5,32,256]{2,1,0:T(8,128)(2,1)S(1)} %get-tuple-element.68), channel_id=1, source_target_pairs={{0,14},{1,15},{2,12},{3,13},{4,10},{5,11},{6,8},{7,9},{8,22},{9,23... | collective-permute-start | bytes 245768 | tf_op jit(solution)/shard_map/ppermute | solution.py:28
  43.5 3.3 %collective-permute-start.18 = (bf16[5,32,256]{2,1,0:T(8,128)(2,1)S(1)}, bf16[5,32,256]{2,1,0:T(8,128)(2,1)S(1)}, u32[]{:S(2)}, u32[]{:S(2)}) collective-permute-start(bf16[5,32,256]{2,1,0:T(8,128)(2,1)S(1)} %get-tuple-element.62.after_ref.refs_13_), channel_id=1, source_target_pairs={{0,8},{1,9},{2,10},{3,11},{4,12},{5,13},{6,14},{7,15},{8,16},{9,17... | collective-permute-start | bytes 245768 | tf_op jit(solution)/shard_map/ppermute | solution.py:28
  47.4 1.7 %collective-permute-done.21.refs_8_ = bf16[5,32,256]{2,1,0:T(8,128)(2,1)S(1)} collective-permute-done((bf16[5,32,256]{2,1,0:T(8,128)(2,1)S(1)}, bf16[5,32,256]{2,1,0:T(8,128)(2,1)S(1)}, u32[]{:S(2)}, u32[]{:S(2)}) %collective-permute-start.21) | collective-permute-done | bytes 81952 | tf_op jit(solution)/shard_map/ppermute | solution.py:28
  53.1 2.1 %collective-permute-start.33 = (bf16[12,32,256]{2,1,0:T(8,128)(2,1)S(1)}, bf16[12,32,256]{2,1,0:T(8,128)(2,1)S(1)}, u32[]{:S(2)}, u32[]{:S(2)}) collective-permute-start(bf16[12,32,256]{2,1,0:T(8,128)(2,1)S(1)} %get-tuple-element.70), channel_id=1, source_target_pairs={{0,2},{1,3},{2,0},{3,1},{4,6},{5,7},{6,4},{7,5},{8,10},{9,11},{10,... | collective-permute-start | bytes 589832 | tf_op jit(solution)/shard_map/ppermute | solution.py:28
  56.8 1.9 %shard_map.60 = (bf16[640,256]{1,0:T(8,128)(2,1)S(1)}, bf16[640,640]{1,0:T(8,128)(2,1)S(1)}, bf16[640,1536]{1,0:T(8,128)(2,1)S(1)}) custom-call(bf16[5,32,256]{2,1,0:T(8,128)(2,1)S(1)} %get-tuple-element.62.after_ref.refs_13_, bf16[4,640,256]{2,1,0:T(8,128)(2,1)} %rhs_hbm.7, bf16[4,640,640]{2,1,0:T(8,128)(2,1)} %inv_hbm.7, bf16[3,12,4,32,640]{4,3,2,1,0:T(8,128)(2,1)} %bitcast.9), custom_call_target="tpu_custom_call" | custom-call | bytes 3112960 | tf_op jit(solution)/shard_map/pallas_call | solution.py:291
  58.7 2.3 %collective-permute-done.33.refs_1_ = bf16[12,32,256]{2,1,0:T(8,128)(2,1)S(1)} collective-permute-done((bf16[12,32,256]{2,1,0:T(8,128)(2,1)S(1)}, bf16[12,32,256]{2,1,0:T(8,128)(2,1)S(1)}, u32[]{:S(2)}, u32[]{:S(2)}) %collective-permute-start.33) | collective-permute-done | bytes 196640 | tf_op jit(solution)/shard_map/ppermute | solution.py:28
  61.6 4.6 %collective-permute-done.34.refs_0_ = bf16[12,32,256]{2,1,0:T(8,128)(2,1)S(1)} collective-permute-done((bf16[12,32,256]{2,1,0:T(8,128)(2,1)S(1)}, bf16[12,32,256]{2,1,0:T(8,128)(2,1)S(1)}, u32[]{:S(2)}, u32[]{:S(2)}) %collective-permute-start.34) | collective-permute-done | bytes 196640 | tf_op jit(solution)/shard_map/ppermute | solution.py:28
  69.1 1.9 %collective-permute-start.38 = (bf16[5,32,256]{2,1,0:T(8,128)(2,1)S(1)}, bf16[5,32,256]{2,1,0:T(8,128)(2,1)S(1)}, u32[]{:S(2)}, u32[]{:S(2)}) collective-permute-start(bf16[5,32,256]{2,1,0:T(8,128)(2,1)S(1)} %get-tuple-element.79), channel_id=1, source_target_pairs={{0,12},{1,13},{2,14},{3,15},{4,8},{5,9},{6,10},{7,11},{8,20},{9,21... | collective-permute-start | bytes 245768 | tf_op jit(solution)/shard_map/ppermute | solution.py:28
  72.2 3.6 %collective-permute-start.39 = (bf16[5,32,256]{2,1,0:T(8,128)(2,1)S(1)}, bf16[5,32,256]{2,1,0:T(8,128)(2,1)S(1)}, u32[]{:S(2)}, u32[]{:S(2)}) collective-permute-start(bf16[5,32,256]{2,1,0:T(8,128)(2,1)S(1)} %get-tuple-element.80), channel_id=1, source_target_pairs={{0,14},{1,15},{2,12},{3,13},{4,10},{5,11},{6,8},{7,9},{8,22},{9,23... | collective-permute-start | bytes 245768 | tf_op jit(solution)/shard_map/ppermute | solution.py:28
  75.8 1.9 %collective-permute-start.36 = (bf16[5,32,256]{2,1,0:T(8,128)(2,1)S(1)}, bf16[5,32,256]{2,1,0:T(8,128)(2,1)S(1)}, u32[]{:S(2)}, u32[]{:S(2)}) collective-permute-start(bf16[5,32,256]{2,1,0:T(8,128)(2,1)S(1)} %get-tuple-element.74.after_ref.refs_13_), channel_id=1, source_target_pairs={{0,8},{1,9},{2,10},{3,11},{4,12},{5,13},{6,14},{7,15},{8,16},{9,17... | collective-permute-start | bytes 245768 | tf_op jit(solution)/shard_map/ppermute | solution.py:28
  78.3 2.0 %collective-permute-done.39.refs_8_ = bf16[5,32,256]{2,1,0:T(8,128)(2,1)S(1)} collective-permute-done((bf16[5,32,256]{2,1,0:T(8,128)(2,1)S(1)}, bf16[5,32,256]{2,1,0:T(8,128)(2,1)S(1)}, u32[]{:S(2)}, u32[]{:S(2)}) %collective-permute-start.39) | collective-permute-done | bytes 81952 | tf_op jit(solution)/shard_map/ppermute | solution.py:28
  80.8 3.1 %collective-permute-done.36.refs_5_ = bf16[5,32,256]{2,1,0:T(8,128)(2,1)S(1)} collective-permute-done((bf16[5,32,256]{2,1,0:T(8,128)(2,1)S(1)}, bf16[5,32,256]{2,1,0:T(8,128)(2,1)S(1)}, u32[]{:S(2)}, u32[]{:S(2)}) %collective-permute-start.36) | collective-permute-done | bytes 81952 | tf_op jit(solution)/shard_map/ppermute | solution.py:28
  91.2 1.9 %shard_map.64 = (bf16[640,256]{1,0:T(8,128)(2,1)S(1)}, bf16[640,640]{1,0:T(8,128)(2,1)S(1)}, bf16[640,1536]{1,0:T(8,128)(2,1)S(1)}) custom-call(bf16[5,32,256]{2,1,0:T(8,128)(2,1)S(1)} %get-tuple-element.74.after_ref.refs_13_, bf16[4,640,256]{2,1,0:T(8,128)(2,1)} %rhs_hbm.7, bf16[4,640,640]{2,1,0:T(8,128)(2,1)} %inv_hbm.7, bf16[3,12,4,32,640]{4,3,2,1,0:T(8,128)(2,1)} %bitcast.10), custom_call_target="tpu_custom_call" | custom-call | bytes 3112960 | tf_op jit(solution)/shard_map/pallas_call | solution.py:291
  94.5 3.3 %collective-permute-done.52.refs_0_ = bf16[12,32,256]{2,1,0:T(8,128)(2,1)S(1)} collective-permute-done((bf16[12,32,256]{2,1,0:T(8,128)(2,1)S(1)}, bf16[12,32,256]{2,1,0:T(8,128)(2,1)S(1)}, u32[]{:S(2)}, u32[]{:S(2)}) %collective-permute-start.52) | collective-permute-done | bytes 196640 | tf_op jit(solution)/shard_map/ppermute | solution.py:28
  97.8 1.8 %shard_map.70 = f32[4,640,256]{2,1,0:T(8,128)} custom-call(s32[1,3]{1,0:T(1,128)S(1)} %bitcast.7, f32[640,256]{1,0:T(8,128)S(1)} %shard_map.66.base_ref, bf16[640,640]{1,0:T(8,128)(2,1)S(1)} %get-tuple-element.83.inv_ref, bf16[640,1536]{1,0:T(8,128)(2,1)S(1)} %get-tuple-element.76.turned_ref, ...), custom_call_target="tpu_custom_call", output_to_operand_aliasing={{}: (6, {})} | custom-call | flops 356515840 | bytes 3997696 | tf_op jit(solution)/shard_map/pallas_call | solution.py:356
  (102 shorter events, 40.4 us)
Async XLA Ops:
  1.6 9.8 %collective-permute-start.4 = (bf16[5,32,256]{2,1,0:T(8,128)(2,1)S(1)}, bf16[5,32,256]{2,1,0:T(8,128)(2,1)S(1)}, u32[]{:S(2)}, u32[]{:S(2)}) collective-permute-start(bf16[5,32,256]{2,1,0:T(8,128)(2,1)S(1)} %get-tuple-element.54), channel_id=1, source_target_pairs={{0,10},{1,11},{2,8},{3,9},{4,14},{5,15},{6,12},{7,13},{8,18},{9,19... | collective-permute-start | bytes 245768 | tf_op jit(solution)/shard_map/ppermute | solution.py:28
  5.7 7.7 %collective-permute-start.5 = (bf16[5,32,256]{2,1,0:T(8,128)(2,1)S(1)}, bf16[5,32,256]{2,1,0:T(8,128)(2,1)S(1)}, u32[]{:S(2)}, u32[]{:S(2)}) collective-permute-start(bf16[5,32,256]{2,1,0:T(8,128)(2,1)S(1)} %get-tuple-element.55), channel_id=1, source_target_pairs={{0,12},{1,13},{2,14},{3,15},{4,8},{5,9},{6,10},{7,11},{8,20},{9,21... | collective-permute-start | bytes 245768 | tf_op jit(solution)/shard_map/ppermute | solution.py:28
  8.2 8.9 %collective-permute-start.6 = (bf16[5,32,256]{2,1,0:T(8,128)(2,1)S(1)}, bf16[5,32,256]{2,1,0:T(8,128)(2,1)S(1)}, u32[]{:S(2)}, u32[]{:S(2)}) collective-permute-start(bf16[5,32,256]{2,1,0:T(8,128)(2,1)S(1)} %get-tuple-element.56), channel_id=1, source_target_pairs={{0,14},{1,15},{2,12},{3,13},{4,10},{5,11},{6,8},{7,9},{8,22},{9,23... | collective-permute-start | bytes 245768 | tf_op jit(solution)/shard_map/ppermute | solution.py:28
  9.7 8.0 %collective-permute-start = (bf16[6,32,256]{2,1,0:T(8,128)(2,1)S(1)}, bf16[6,32,256]{2,1,0:T(8,128)(2,1)S(1)}, u32[]{:S(2)}, u32[]{:S(2)}) collective-permute-start(bf16[6,32,256]{2,1,0:T(8,128)(2,1)S(1)} %get-tuple-element.51), channel_id=1, source_target_pairs={{0,2},{1,3},{2,0},{3,1},{4,6},{5,7},{6,4},{7,5},{8,10},{9,11},{10,... | collective-permute-start | bytes 294920 | tf_op jit(solution)/shard_map/ppermute | solution.py:28
  11.4 7.6 %collective-permute-start.1 = (bf16[6,32,256]{2,1,0:T(8,128)(2,1)S(1)}, bf16[6,32,256]{2,1,0:T(8,128)(2,1)S(1)}, u32[]{:S(2)}, u32[]{:S(2)}) collective-permute-start(bf16[6,32,256]{2,1,0:T(8,128)(2,1)S(1)} %get-tuple-element.52), channel_id=1, source_target_pairs={{0,4},{1,5},{2,6},{3,7},{4,0},{5,1},{6,2},{7,3},{8,12},{9,13},{10,... | collective-permute-start | bytes 294920 | tf_op jit(solution)/shard_map/ppermute | solution.py:28
  21.6 7.8 %collective-permute-start.15 = (bf16[12,32,256]{2,1,0:T(8,128)(2,1)S(1)}, bf16[12,32,256]{2,1,0:T(8,128)(2,1)S(1)}, u32[]{:S(2)}, u32[]{:S(2)}) collective-permute-start(bf16[12,32,256]{2,1,0:T(8,128)(2,1)S(1)} %get-tuple-element.58), channel_id=1, source_target_pairs={{0,2},{1,3},{2,0},{3,1},{4,6},{5,7},{6,4},{7,5},{8,10},{9,11},{10,... | collective-permute-start | bytes 589832 | tf_op jit(solution)/shard_map/ppermute | solution.py:28
  22.0 10.3 %collective-permute-start.16 = (bf16[12,32,256]{2,1,0:T(8,128)(2,1)S(1)}, bf16[12,32,256]{2,1,0:T(8,128)(2,1)S(1)}, u32[]{:S(2)}, u32[]{:S(2)}) collective-permute-start(bf16[12,32,256]{2,1,0:T(8,128)(2,1)S(1)} %get-tuple-element.60), channel_id=1, source_target_pairs={{0,4},{1,5},{2,6},{3,7},{4,0},{5,1},{6,2},{7,3},{8,12},{9,13},{10,... | collective-permute-start | bytes 589832 | tf_op jit(solution)/shard_map/ppermute | solution.py:28
  23.4 10.6 %collective-permute-start.17 = (bf16[12,32,256]{2,1,0:T(8,128)(2,1)S(1)}, bf16[12,32,256]{2,1,0:T(8,128)(2,1)S(1)}, u32[]{:S(2)}, u32[]{:S(2)}) collective-permute-start(bf16[12,32,256]{2,1,0:T(8,128)(2,1)S(1)} %get-tuple-element.61), channel_id=1, source_target_pairs={{0,6},{1,7},{2,4},{3,5},{4,2},{5,3},{6,0},{7,1},{8,14},{9,15},{10,... | collective-permute-start | bytes 589832 | tf_op jit(solution)/shard_map/ppermute | solution.py:28
  35.8 7.7 %collective-permute-start.19 = (bf16[5,32,256]{2,1,0:T(8,128)(2,1)S(1)}, bf16[5,32,256]{2,1,0:T(8,128)(2,1)S(1)}, u32[]{:S(2)}, u32[]{:S(2)}) collective-permute-start(bf16[5,32,256]{2,1,0:T(8,128)(2,1)S(1)} %get-tuple-element.66), channel_id=1, source_target_pairs={{0,10},{1,11},{2,8},{3,9},{4,14},{5,15},{6,12},{7,13},{8,18},{9,19... | collective-permute-start | bytes 245768 | tf_op jit(solution)/shard_map/ppermute | solution.py:28
  37.8 9.1 %collective-permute-start.20 = (bf16[5,32,256]{2,1,0:T(8,128)(2,1)S(1)}, bf16[5,32,256]{2,1,0:T(8,128)(2,1)S(1)}, u32[]{:S(2)}, u32[]{:S(2)}) collective-permute-start(bf16[5,32,256]{2,1,0:T(8,128)(2,1)S(1)} %get-tuple-element.67), channel_id=1, source_target_pairs={{0,12},{1,13},{2,14},{3,15},{4,8},{5,9},{6,10},{7,11},{8,20},{9,21... | collective-permute-start | bytes 245768 | tf_op jit(solution)/shard_map/ppermute | solution.py:28
  39.6 7.3 %collective-permute-start.28 = (bf16[5,32,256]{2,1,0:T(8,128)(2,1)S(1)}, bf16[5,32,256]{2,1,0:T(8,128)(2,1)S(1)}, u32[]{:S(2)}, u32[]{:S(2)}) collective-permute-start(bf16[5,32,256]{2,1,0:T(8,128)(2,1)S(1)} %get-tuple-element.68), channel_id=1, source_target_pairs={{0,6},{1,7},{2,4},{3,5},{4,2},{5,3},{6,0},{7,1},{8,14},{9,15},{10,... | collective-permute-start | bytes 245768 | tf_op jit(solution)/shard_map/ppermute | solution.py:28
  41.0 8.0 %collective-permute-start.21 = (bf16[5,32,256]{2,1,0:T(8,128)(2,1)S(1)}, bf16[5,32,256]{2,1,0:T(8,128)(2,1)S(1)}, u32[]{:S(2)}, u32[]{:S(2)}) collective-permute-start(bf16[5,32,256]{2,1,0:T(8,128)(2,1)S(1)} %get-tuple-element.68), channel_id=1, source_target_pairs={{0,14},{1,15},{2,12},{3,13},{4,10},{5,11},{6,8},{7,9},{8,22},{9,23... | collective-permute-start | bytes 245768 | tf_op jit(solution)/shard_map/ppermute | solution.py:28
  43.5 7.6 %collective-permute-start.18 = (bf16[5,32,256]{2,1,0:T(8,128)(2,1)S(1)}, bf16[5,32,256]{2,1,0:T(8,128)(2,1)S(1)}, u32[]{:S(2)}, u32[]{:S(2)}) collective-permute-start(bf16[5,32,256]{2,1,0:T(8,128)(2,1)S(1)} %get-tuple-element.62.after_ref.refs_13_), channel_id=1, source_target_pairs={{0,8},{1,9},{2,10},{3,11},{4,12},{5,13},{6,14},{7,15},{8,16},{9,17... | collective-permute-start | bytes 245768 | tf_op jit(solution)/shard_map/ppermute | solution.py:28
  53.1 7.9 %collective-permute-start.33 = (bf16[12,32,256]{2,1,0:T(8,128)(2,1)S(1)}, bf16[12,32,256]{2,1,0:T(8,128)(2,1)S(1)}, u32[]{:S(2)}, u32[]{:S(2)}) collective-permute-start(bf16[12,32,256]{2,1,0:T(8,128)(2,1)S(1)} %get-tuple-element.70), channel_id=1, source_target_pairs={{0,2},{1,3},{2,0},{3,1},{4,6},{5,7},{6,4},{7,5},{8,10},{9,11},{10,... | collective-permute-start | bytes 589832 | tf_op jit(solution)/shard_map/ppermute | solution.py:28
  55.3 10.9 %collective-permute-start.34 = (bf16[12,32,256]{2,1,0:T(8,128)(2,1)S(1)}, bf16[12,32,256]{2,1,0:T(8,128)(2,1)S(1)}, u32[]{:S(2)}, u32[]{:S(2)}) collective-permute-start(bf16[12,32,256]{2,1,0:T(8,128)(2,1)S(1)} %get-tuple-element.72), channel_id=1, source_target_pairs={{0,4},{1,5},{2,6},{3,7},{4,0},{5,1},{6,2},{7,3},{8,12},{9,13},{10,... | collective-permute-start | bytes 589832 | tf_op jit(solution)/shard_map/ppermute | solution.py:28
  56.1 10.0 %collective-permute-start.35 = (bf16[12,32,256]{2,1,0:T(8,128)(2,1)S(1)}, bf16[12,32,256]{2,1,0:T(8,128)(2,1)S(1)}, u32[]{:S(2)}, u32[]{:S(2)}) collective-permute-start(bf16[12,32,256]{2,1,0:T(8,128)(2,1)S(1)} %get-tuple-element.73), channel_id=1, source_target_pairs={{0,6},{1,7},{2,4},{3,5},{4,2},{5,3},{6,0},{7,1},{8,14},{9,15},{10,... | collective-permute-start | bytes 589832 | tf_op jit(solution)/shard_map/ppermute | solution.py:28
  67.9 7.9 %collective-permute-start.37 = (bf16[5,32,256]{2,1,0:T(8,128)(2,1)S(1)}, bf16[5,32,256]{2,1,0:T(8,128)(2,1)S(1)}, u32[]{:S(2)}, u32[]{:S(2)}) collective-permute-start(bf16[5,32,256]{2,1,0:T(8,128)(2,1)S(1)} %get-tuple-element.78), channel_id=1, source_target_pairs={{0,10},{1,11},{2,8},{3,9},{4,14},{5,15},{6,12},{7,13},{8,18},{9,19... | collective-permute-start | bytes 245768 | tf_op jit(solution)/shard_map/ppermute | solution.py:28
  67.9 7.9 %collective-permute-start.45 = (bf16[5,32,256]{2,1,0:T(8,128)(2,1)S(1)}, bf16[5,32,256]{2,1,0:T(8,128)(2,1)S(1)}, u32[]{:S(2)}, u32[]{:S(2)}) collective-permute-start(bf16[5,32,256]{2,1,0:T(8,128)(2,1)S(1)} %get-tuple-element.79), channel_id=1, source_target_pairs={{0,4},{1,5},{2,6},{3,7},{4,0},{5,1},{6,2},{7,3},{8,12},{9,13},{10,... | collective-permute-start | bytes 245768 | tf_op jit(solution)/shard_map/ppermute | solution.py:28
  69.1 8.7 %collective-permute-start.38 = (bf16[5,32,256]{2,1,0:T(8,128)(2,1)S(1)}, bf16[5,32,256]{2,1,0:T(8,128)(2,1)S(1)}, u32[]{:S(2)}, u32[]{:S(2)}) collective-permute-start(bf16[5,32,256]{2,1,0:T(8,128)(2,1)S(1)} %get-tuple-element.79), channel_id=1, source_target_pairs={{0,12},{1,13},{2,14},{3,15},{4,8},{5,9},{6,10},{7,11},{8,20},{9,21... | collective-permute-start | bytes 245768 | tf_op jit(solution)/shard_map/ppermute | solution.py:28
  72.2 8.0 %collective-permute-start.39 = (bf16[5,32,256]{2,1,0:T(8,128)(2,1)S(1)}, bf16[5,32,256]{2,1,0:T(8,128)(2,1)S(1)}, u32[]{:S(2)}, u32[]{:S(2)}) collective-permute-start(bf16[5,32,256]{2,1,0:T(8,128)(2,1)S(1)} %get-tuple-element.80), channel_id=1, source_target_pairs={{0,14},{1,15},{2,12},{3,13},{4,10},{5,11},{6,8},{7,9},{8,22},{9,23... | collective-permute-start | bytes 245768 | tf_op jit(solution)/shard_map/ppermute | solution.py:28
  75.8 8.1 %collective-permute-start.36 = (bf16[5,32,256]{2,1,0:T(8,128)(2,1)S(1)}, bf16[5,32,256]{2,1,0:T(8,128)(2,1)S(1)}, u32[]{:S(2)}, u32[]{:S(2)}) collective-permute-start(bf16[5,32,256]{2,1,0:T(8,128)(2,1)S(1)} %get-tuple-element.74.after_ref.refs_13_), channel_id=1, source_target_pairs={{0,8},{1,9},{2,10},{3,11},{4,12},{5,13},{6,14},{7,15},{8,16},{9,17... | collective-permute-start | bytes 245768 | tf_op jit(solution)/shard_map/ppermute | solution.py:28
  85.9 8.0 %collective-permute-start.51 = (bf16[12,32,256]{2,1,0:T(8,128)(2,1)S(1)}, bf16[12,32,256]{2,1,0:T(8,128)(2,1)S(1)}, u32[]{:S(2)}, u32[]{:S(2)}) collective-permute-start(bf16[12,32,256]{2,1,0:T(8,128)(2,1)S(1)} %get-tuple-element.82), channel_id=1, source_target_pairs={{0,2},{1,3},{2,0},{3,1},{4,6},{5,7},{6,4},{7,5},{8,10},{9,11},{10,... | collective-permute-start | bytes 589832 | tf_op jit(solution)/shard_map/ppermute | solution.py:28
  86.9 10.9 %collective-permute-start.52 = (bf16[12,32,256]{2,1,0:T(8,128)(2,1)S(1)}, bf16[12,32,256]{2,1,0:T(8,128)(2,1)S(1)}, u32[]{:S(2)}, u32[]{:S(2)}) collective-permute-start(bf16[12,32,256]{2,1,0:T(8,128)(2,1)S(1)} %get-tuple-element.84), channel_id=1, source_target_pairs={{0,4},{1,5},{2,6},{3,7},{4,0},{5,1},{6,2},{7,3},{8,12},{9,13},{10,... | collective-permute-start | bytes 589832 | tf_op jit(solution)/shard_map/ppermute | solution.py:28
  87.8 9.9 %collective-permute-start.53 = (bf16[12,32,256]{2,1,0:T(8,128)(2,1)S(1)}, bf16[12,32,256]{2,1,0:T(8,128)(2,1)S(1)}, u32[]{:S(2)}, u32[]{:S(2)}) collective-permute-start(bf16[12,32,256]{2,1,0:T(8,128)(2,1)S(1)} %get-tuple-element.85), channel_id=1, source_target_pairs={{0,6},{1,7},{2,4},{3,5},{4,2},{5,3},{6,0},{7,1},{8,14},{9,15},{10,... | collective-permute-start | bytes 589832 | tf_op jit(solution)/shard_map/ppermute | solution.py:28
  (31 other events, 110.3 us)
